TPU v7x, 512 devices: a whole 4x8x8 slice. The times are simulated.
512 devices in a mesh: ctx: 128 (over y_lo, z, x), head: 4 (over y_hi, core).
Axes of the slice: x: 4, y: 8 (y_hi: 2, y_lo: 4; y = y_hi * 4 + y_lo), z: 8, core: 2. Of those that a mesh axis runs over, the one named last changes fastest.
Arguments:
- queries: bfloat16 [65536, 1024], P('ctx', 'head'), may hold values from -40 to 40
- keys: bfloat16 [65536, 1024], P('ctx', 'head'), may hold values from -40 to 40
- values: bfloat16 [65536, 1024], P('ctx', 'head'), may hold values from -6 to 6
- out_weight: bfloat16 [1024, 1024], P('head'), may hold values from -0.1875 to 0.1875
- grad_output: bfloat16 [65536, 1024], P('ctx', 'head'), may hold values from -6 to 6
- key_lists: int32 [512, 8], replicated, may hold values from 0 to 511, as said below
- key_counts: int32 [512], replicated, may hold values from 1 to 8, as said below
Outputs:
- output: bfloat16 [65536, 1024], P('ctx', 'head')
- grad_queries: bfloat16 [65536, 1024], P('ctx', 'head')
- grad_keys: bfloat16 [65536, 1024], P('ctx', 'head')
- grad_values: bfloat16 [65536, 1024], P('ctx', 'head')
- grad_weight: float32 [1024, 1024], P('head')
Inputs may be any that keep to these rules, and one draw needn't show every extreme that they name: `key_lists`: row a names 8 different key blocks, all among the 12 blocks from 4 * (a // 4 - 1) on, counted modulo 512; its first entry is a itself, its second lies among the first 4 of those blocks, its third among the last 4. `key_counts`: every query block whose index is a multiple of 4 uses all 8 slots.
All inputs are finite; a program needn't handle non-finite values.
Results may differ from a plain program's by a relative error of at most 0.029.
Values may be sent and summed in bfloat16 or wider, within the bound.
A program may use at most 128 MiB of HBM per device.

v0:
```python
import jax
import jax.numpy as jnp
from jax import lax
from jax.sharding import PartitionSpec as P

HD = 128
BLK = 128


def with_halo(block, sides, width):
    for axis, dim in sides:
        count = lax.axis_size(axis)
        forward = [(i, i + 1) for i in range(count - 1)]
        forward.append((count - 1, 0))
        backward = [(target, source) for source, target in forward]
        low = lax.ppermute(
            lax.slice_in_dim(block, block.shape[dim] - width, None, axis=dim), axis, forward
        )
        high = lax.ppermute(lax.slice_in_dim(block, 0, width, axis=dim), axis, backward)
        block = jnp.concatenate([low, block, high], axis=dim)
    return block


def block_scores(query_sel, key_sel, usable, factor):
    scores = (
        jnp.einsum("nihd,nsjhd->nhisj", query_sel, key_sel, preferred_element_type=jnp.float32)
        * factor
    )
    return jnp.where(usable[:, None, None, :, None], scores, -jnp.inf)


def key_side(query_sel, grad_sel, log_total, row_dots, picks, usable, window, factor):
    span = window.shape[1]
    key_sel = window[0][picks]
    value_sel = window[1][picks]
    scores = block_scores(query_sel, key_sel, usable, factor)
    probs = jnp.exp(scores - log_total)
    prob_half = probs.astype(jnp.bfloat16)
    grad_probs = jnp.einsum(
        "nihd,nsjhd->nhisj", grad_sel, value_sel, preferred_element_type=jnp.float32
    )
    grad_scores = (probs * (grad_probs - row_dots) * factor).astype(jnp.bfloat16)
    key_parts = jnp.einsum(
        "nhisj,nihd->nsjhd", grad_scores, query_sel, preferred_element_type=jnp.float32
    )
    value_parts = jnp.einsum(
        "nhisj,nihd->nsjhd", prob_half, grad_sel, preferred_element_type=jnp.float32
    )
    selector = (picks[:, :, None] == jnp.arange(span, dtype=jnp.int32)[None, None, :]).astype(
        jnp.float32
    )
    key_window = jnp.einsum("nsw,nsjhd->wjhd", selector, key_parts, precision=lax.Precision.HIGHEST)
    value_window = jnp.einsum(
        "nsw,nsjhd->wjhd", selector, value_parts, precision=lax.Precision.HIGHEST
    )
    query_grad = None
    query_grad = jnp.einsum(
        "nhisj,nsjhd->nihd", grad_scores, key_sel, preferred_element_type=jnp.float32
    )
    return (query_grad, key_window, value_window)


def shards(queries, keys, values, out_weight, grad_output, key_lists, key_counts):
    tok_rows, features = queries.shape
    heads_here = features // HD
    blocks = tok_rows // BLK
    cycle_size = lax.axis_size("ctx")
    cycle_pos = lax.axis_index("ctx")
    all_blocks = blocks * cycle_size
    factor = HD ** (-0.5)
    window_start = (cycle_pos - 1) * blocks
    slot_ids = jnp.arange(key_lists.shape[1], dtype=jnp.int32)
    stacked = jnp.stack([keys, values])
    window = with_halo(stacked, (("ctx", 1),), tok_rows)
    window = window.reshape(2, 3 * blocks, BLK, heads_here, HD)
    own_lists = lax.dynamic_slice_in_dim(key_lists, cycle_pos * blocks, blocks, 0)
    own_counts = lax.dynamic_slice_in_dim(key_counts, cycle_pos * blocks, blocks, 0)
    picks = (own_lists - window_start) % all_blocks
    usable = slot_ids[None, :] < own_counts[:, None]
    query_sel = queries.reshape(blocks, BLK, heads_here, HD)
    key_sel = window[0][picks]
    value_sel = window[1][picks]
    scores = block_scores(query_sel, key_sel, usable, factor)
    top_score = jnp.max(scores, axis=(3, 4), keepdims=True)
    log_total = top_score + jnp.log(
        jnp.sum(jnp.exp(scores - top_score), axis=(3, 4), keepdims=True)
    )
    prob_half = jnp.exp(scores - log_total).astype(jnp.bfloat16)
    mixed = jnp.einsum(
        "nhisj,nsjhd->nihd", prob_half, value_sel, preferred_element_type=jnp.float32
    )
    attn = mixed.astype(jnp.bfloat16).reshape(tok_rows, features)
    partial_out = jnp.dot(attn, out_weight, preferred_element_type=jnp.float32)
    output = lax.psum_scatter(
        partial_out.astype(jnp.bfloat16), "head", scatter_dimension=1, tiled=True
    )
    column_block = lax.all_gather(grad_output, "head", axis=1, tiled=True)
    back_sum = lax.dot_general(
        column_block, out_weight, (((1,), (1,)), ((), ())), preferred_element_type=jnp.float32
    )
    product = lax.dot_general(
        attn, column_block, (((0,), (0,)), ((), ())), preferred_element_type=jnp.float32
    )
    weight_part = product
    back_sum, weight_part = (back_sum, weight_part)
    grad_attn = back_sum.astype(jnp.bfloat16)
    grad_weight = lax.psum(weight_part, "ctx") * (cycle_size * tok_rows) ** (-0.5)
    dots_rows = jnp.sum(
        (grad_attn.astype(jnp.float32) * attn.astype(jnp.float32)).reshape(
            blocks, BLK, heads_here, HD
        ),
        axis=3,
    )
    row_dots = jnp.transpose(dots_rows, (0, 2, 1))
    grad_sel = grad_attn.reshape(blocks, BLK, heads_here, HD)
    query_grad, key_window, value_window = key_side(
        query_sel, grad_sel, log_total, row_dots[..., None, None], picks, usable, window, factor
    )
    parts = jnp.stack([key_window, value_window]).reshape(2, 3 * tok_rows, features)
    outgoing = jnp.concatenate([parts[:, :tok_rows], parts[:, 2 * tok_rows :]], axis=1)
    returned = with_halo(outgoing.astype(jnp.bfloat16), (("ctx", 1),), tok_rows).astype(
        outgoing.dtype
    )
    summed = (
        parts[:, tok_rows : 2 * tok_rows] + returned[:, :tok_rows] + returned[:, 3 * tok_rows :]
    )
    grad_queries = query_grad.astype(jnp.bfloat16).reshape(tok_rows, features)
    return (
        output,
        grad_queries,
        summed[0].astype(jnp.bfloat16),
        summed[1].astype(jnp.bfloat16),
        grad_weight,
    )


def solution(mesh):
    in_specs = (
        P("ctx", "head"),
        P("ctx", "head"),
        P("ctx", "head"),
        P("head", None),
        P("ctx", "head"),
        P(),
        P(),
    )
    out_specs = (
        P("ctx", "head"),
        P("ctx", "head"),
        P("ctx", "head"),
        P("ctx", "head"),
        P("head", None),
    )
    return jax.shard_map(shards, mesh=mesh, in_specs=in_specs, out_specs=out_specs, check_vma=False)
```

profile of v0, /device:TPU:1, one launch (start us, length us, event | category | flops | bytes accessed | tf_op | source)
XLA Modules:
  0.0 1521.0 jit_solution(13848686088322686744)
XLA Ops:
  8.4 16.7 %collective-permute-start.1 = (bf16[2,512,256]{2,1,0:T(8,128)(2,1)S(1)}, bf16[2,512,256]{2,1,0:T(8,128)(2,1)S(1)}, u32[]{:S(2)}, u32[]{:S(2)}) collective-permute-start(bf16[2,512,256]{2,1,0:T(8,128)(2,1)S(1)} %pad_maximum_fusion.4), channel_id=1, source_target_pairs={{4,0},{8,4},{12,8},{16,12},{20,16},{24,20},{28,24},{32,28},{36,32}... | collective-permute-start | bytes 1572872 | tf_op jit(solution)/shard_map/ppermute | solution.py:19
  25.1 1.9 collective-permute-start
  28.8 1.7 reshape.68
  30.6 5.1 collective-permute-done.1
  35.7 9.8 collective-permute-done
  47.9 2.0 squeeze.5
  50.1 2.2 gather_fusion.1
  52.4 2.1 gather_fusion
  54.5 1.7 bitcast_reduce_fusion
  61.5 2.7 fusion.45
  67.5 5.1 fusion.8
  75.4 1.7 fusion.19
  77.1 2.0 copy.94
  79.1 2.5 stack.21
  81.7 3.4 fusion.22
  85.1 2.0 copy.97
  87.1 3.3 stack.22
  92.1 1.5 copy-done.3
  93.6 2.1 collective-permute-start.2
  95.7 9.4 collective-permute-start.3
  106.8 6.6 collective-permute-done.2
  116.5 1265.3 %all-reduce.2.cloned.1.call-done = f32[256,1024]{1,0:T(8,128)} async-done(((f32[256,1024]{1,0:T(8,128)}), f32[256,1024]{1,0:T(8,128)}) %all-reduce.2.cloned.1.call-update) | async-done | bytes 1048592 | tf_op jit(solution)/shard_map/psum | solution.py:107
  1381.8 2.3 broadcast_multiply_fusion
  1384.1 130.3 %reduce-scatter.2.cloned.1.call-done = bf16[512,256]{1,0:T(8,128)(2,1)} async-done(((bf16[512,1024]{1,0:T(8,128)(2,1)}), bf16[512,256]{1,0:T(8,128)(2,1)}) %reduce-scatter.2.cloned.1.call-update) | async-done | bytes 262160 | tf_op jit(solution)/shard_map/reduce_scatter | solution.py:94
  (70 shorter events, 23.5 us)
Async XLA Ops:
  7.2 57.3 %copy-start = (bf16[256,1024]{1,0:T(8,128)(2,1)S(1)}, bf16[256,1024]{1,0:T(8,128)(2,1)}, u32[]{:S(2)}) copy-start(bf16[256,1024]{1,0:T(8,128)(2,1)} %param.10) | copy-start | bytes 1572868
  7.2 54.3 %all-gather.2.cloned.1.call-start = ((), (), s32[]{:S(2)}) async-start(), calls=%async_computation.2 | async-start | bytes 1310720 | tf_op jit(solution)/shard_map/all_gather | solution.py:97
  8.4 27.3 %collective-permute-start.1 = (bf16[2,512,256]{2,1,0:T(8,128)(2,1)S(1)}, bf16[2,512,256]{2,1,0:T(8,128)(2,1)S(1)}, u32[]{:S(2)}, u32[]{:S(2)}) collective-permute-start(bf16[2,512,256]{2,1,0:T(8,128)(2,1)S(1)} %pad_maximum_fusion.4), channel_id=1, source_target_pairs={{4,0},{8,4},{12,8},{16,12},{20,16},{24,20},{28,24},{32,28},{36,32}... | collective-permute-start | bytes 1572872 | tf_op jit(solution)/shard_map/ppermute | solution.py:19
  25.1 20.4 %collective-permute-start = (bf16[2,512,256]{2,1,0:T(8,128)(2,1)S(1)}, bf16[2,512,256]{2,1,0:T(8,128)(2,1)S(1)}, u32[]{:S(2)}, u32[]{:S(2)}) collective-permute-start(bf16[2,512,256]{2,1,0:T(8,128)(2,1)S(1)} %pad_maximum_fusion.4), channel_id=1, source_target_pairs={{0,4},{4,8},{8,12},{12,16},{16,20},{20,24},{24,28},{28,32},{32,36}... | collective-permute-start | bytes 1572872 | tf_op jit(solution)/shard_map/ppermute | solution.py:16
  27.1 1354.7 %all-reduce.2.cloned.1.call-start = ((), (), s32[]{:S(2)}) async-start(), calls=%async_computation.3 | async-start | bytes 2097152 | tf_op jit(solution)/shard_map/psum | solution.py:107
  52.3 2.1 copy-start.8
  56.2 2.0 copy-start.1
  58.1 2.3 copy-start.10
  59.1 1.3 copy-start.12
  64.1 1.8 copy-start.5
  64.2 1450.3 %reduce-scatter.2.cloned.1.call-start = ((), (), s32[]{:S(2)}) async-start(), calls=%async_computation.1 | async-start | bytes 1310720 | tf_op jit(solution)/shard_map/reduce_scatter | solution.py:94
  67.5 5.1 copy-start.2
  67.5 5.1 copy-start.11
  72.6 1.4 copy-start.13
  74.0 1.3 copy-start.6
  90.4 1.4 copy-start.4
  91.9 1.6 copy-start.3
  91.9 13.2 copy-start.9
  93.6 11.5 copy-start.7
  93.6 19.8 %collective-permute-start.2 = (bf16[2,512,256]{2,1,0:T(8,128)(2,1)S(1)}, bf16[2,512,256]{2,1,0:T(8,128)(2,1)S(1)}, u32[]{:S(2)}, u32[]{:S(2)}) collective-permute-start(bf16[2,512,256]{2,1,0:T(8,128)(2,1)S(1)} %get-tuple-element.7), channel_id=1, source_target_pairs={{0,4},{4,8},{8,12},{12,16},{16,20},{20,24},{24,28},{28,32},{32,36}... | collective-permute-start | bytes 1572872 | tf_op jit(solution)/shard_map/ppermute | solution.py:16
  95.7 18.7 %collective-permute-start.3 = (bf16[2,512,256]{2,1,0:T(8,128)(2,1)S(1)}, bf16[2,512,256]{2,1,0:T(8,128)(2,1)S(1)}, u32[]{:S(2)}, u32[]{:S(2)}) collective-permute-start(bf16[2,512,256]{2,1,0:T(8,128)(2,1)S(1)} %get-tuple-element.8), channel_id=1, source_target_pairs={{4,0},{8,4},{12,8},{16,12},{20,16},{24,20},{28,24},{32,28},{36,32}... | collective-permute-start | bytes 1572872 | tf_op jit(solution)/shard_map/ppermute | solution.py:19
Sparse Core Ops, SparseCore 0:
  27.2 31.4 all-gather.1
  64.3 1317.4 all-reduce.1
  1385.7 128.6 reduce-scatter.1
where the time goes:
time: 1520 us
  waiting for transfers between devices  1420 us (93%)
  starting transfers between devices  30.4 us (2%)
  local copies, waits for them, and re-layouts  28.1 us (2%)
  matrix products  20.8 us (1%)
    psum x1, waiting for transfers between devices, shards(): lax.psum(weight_part, 'ctx') * (cycle_size * tok_rows) ** (-0.5)  1270 us
    reduce_scatter x1, waiting for transfers between devices, shards(): lax.psum_scatter(partial_out.astype(jnp.bfloat16), 'head', scatter_dimens...  130 us
  transfers between devices with their start and end apart: 7, of which 6 were waited for; matrix products, arithmetic and copies ran while one was open for 3% of the time, Pallas kernels for 0%

commit v1 on v0

--- a/solution.py
+++ b/solution.py
@@ -1,10 +1,140 @@
+import functools
+
 import jax
 import jax.numpy as jnp
 from jax import lax
+from jax.experimental import pallas as pl
+from jax.experimental.pallas import tpu as pltpu
 from jax.sharding import PartitionSpec as P
 
 HD = 128
 BLK = 128
+MESH = pl.DeviceIdType.MESH
+NY, NZ, NX = 4, 8, 4
+
+
+def spots():
+    pos = lax.axis_index("ctx")
+    x = pos % NX
+    z = (pos // NX) % NZ
+    y = pos // (NX * NZ)
+    return y, z, x
+
+
+def x_peer(d):
+    y, z, x = spots()
+    p = (x + d) % NX
+    return p, {"ctx": (y * NZ + z) * NX + p, "head": lax.axis_index("head")}
+
+
+def z_peer(d):
+    y, z, x = spots()
+    p = (z + d) % NZ
+    return p, {"ctx": (y * NZ + p) * NX + x, "head": lax.axis_index("head")}
+
+
+def y_peer(d):
+    y, z, x = spots()
+    p = (y + d) % NY
+    return p, {"ctx": (p * NZ + z) * NX + x, "head": lax.axis_index("head")}
+
+
+def remote(src, dst, sems, k, device):
+    return pltpu.make_async_remote_copy(
+        src_ref=src,
+        dst_ref=dst,
+        send_sem=sems.at[0, k],
+        recv_sem=sems.at[1, k],
+        device_id=device,
+        device_id_type=MESH,
+    )
+
+
+def sum_kernel(scale, part_ref, out_ref, part, xr, s1, zr, s2, yr, gy, gz, gx, sx, sz, sy, ty, tz, tx):
+    y, z, x = spots()
+    barrier = pltpu.get_barrier_semaphore()
+    peers = [x_peer(d) for d in range(1, NX)] + [z_peer(d) for d in range(1, NZ)]
+    peers += [y_peer(d) for d in range(1, NY)]
+    for _, device in peers:
+        pl.semaphore_signal(barrier, inc=1, device_id=device, device_id_type=MESH)
+    part[...] = part_ref[...].astype(jnp.bfloat16)
+    pl.semaphore_wait(barrier, len(peers))
+
+    def run(copies):
+        for c in copies:
+            c.start()
+        for c in copies:
+            c.wait()
+
+    rows = lambda i, n: pl.ds(pl.multiple_of(i * n, n), n)
+    f32 = jnp.float32
+    copies = []
+    for d in range(1, NX):
+        p, device = x_peer(d)
+        copies.append(remote(part.at[rows(p, 64)], xr.at[d - 1], sx, d - 1, device))
+    run(copies)
+    total = part_ref[rows(x, 64)]
+    for d in range(NX - 1):
+        total = total + xr[d].astype(f32)
+    s1[...] = total.astype(jnp.bfloat16)
+    copies = []
+    for d in range(1, NZ):
+        p, device = z_peer(d)
+        copies.append(remote(s1.at[:, rows(p, 128)], zr.at[d - 1], sz, d - 1, device))
+    run(copies)
+    total = s1[:, rows(z, 128)].astype(f32)
+    for d in range(NZ - 1):
+        total = total + zr[d].astype(f32)
+    s2[...] = total.astype(jnp.bfloat16)
+    copies = []
+    for d in range(1, NY):
+        p, device = y_peer(d)
+        copies.append(remote(s2.at[rows(p, 16)], yr.at[d - 1], sy, d - 1, device))
+    run(copies)
+    total = s2[rows(y, 16)].astype(f32)
+    for d in range(NY - 1):
+        total = total + yr[d].astype(f32)
+    gy[rows(y, 16)] = total.astype(jnp.bfloat16)
+    run([
+        remote(gy.at[rows(y, 16)], gy.at[rows(y, 16)], ty, d - 1, y_peer(d)[1])
+        for d in range(1, NY)
+    ])
+    gz[:, rows(z, 128)] = gy[...]
+    run([
+        remote(gy, gz.at[:, rows(z, 128)], tz, d - 1, z_peer(d)[1])
+        for d in range(1, NZ)
+    ])
+    gx[rows(x, 64)] = gz[...]
+    run([
+        remote(gz, gx.at[rows(x, 64)], tx, d - 1, x_peer(d)[1])
+        for d in range(1, NX)
+    ])
+    out_ref[...] = gx[...].astype(f32) * scale
+
+
+def ctx_sum(part, scale):
+    bf = jnp.bfloat16
+    dma = lambda n: pltpu.SemaphoreType.DMA((2, n))
+    return pl.pallas_call(
+        functools.partial(sum_kernel, scale),
+        out_shape=jax.ShapeDtypeStruct(part.shape, jnp.float32),
+        in_specs=[pl.BlockSpec(memory_space=pltpu.VMEM)],
+        out_specs=pl.BlockSpec(memory_space=pltpu.VMEM),
+        scratch_shapes=[
+            pltpu.VMEM((256, 1024), bf),
+            pltpu.VMEM((NX - 1, 64, 1024), bf),
+            pltpu.VMEM((64, 1024), bf),
+            pltpu.VMEM((NZ - 1, 64, 128), bf),
+            pltpu.VMEM((64, 128), bf),
+            pltpu.VMEM((NY - 1, 16, 128), bf),
+            pltpu.VMEM((64, 128), bf),
+            pltpu.VMEM((64, 1024), bf),
+            pltpu.VMEM((256, 1024), bf),
+            dma(NX - 1), dma(NZ - 1), dma(NY - 1), dma(NY - 1), dma(NZ - 1), dma(NX - 1),
+        ],
+        compiler_params=pltpu.CompilerParams(collective_id=0, has_side_effects=True),
+        name="ctx_sum",
+    )(part)
 
 
 def with_halo(block, sides, width):
@@ -104,7 +234,7 @@
     weight_part = product
     back_sum, weight_part = (back_sum, weight_part)
     grad_attn = back_sum.astype(jnp.bfloat16)
-    grad_weight = lax.psum(weight_part, "ctx") * (cycle_size * tok_rows) ** (-0.5)
+    grad_weight = ctx_sum(weight_part, (cycle_size * tok_rows) ** (-0.5))
     dots_rows = jnp.sum(
         (grad_attn.astype(jnp.float32) * attn.astype(jnp.float32)).reshape(
             blocks, BLK, heads_here, HD

time: 1520 us -> 166 us (0.11)
  the two profiles are of different devices: /device:TPU:1 before, /device:TPU:4 now
where the time goes in v1:
time: 166 us; the launch traced here: 165 us
  Pallas kernels  58 us (35%)
  local copies, waits for them, and re-layouts  31.1 us (19%)
  matrix products  23 us (14%)
  waiting for transfers between devices  18.5 us (11%)
  between operations  14.4 us (9%)
  starting transfers between devices  12.8 us (8%)
  other arithmetic  7.6 us (5%)
    pallas_call x1, Pallas kernels, ctx_sum(): pl.pallas_call(functools.partial(sum_kernel, scale), out_shape=jax.ShapeD...  58 us
    all_gather x1, waiting for transfers between devices, shards(): column_block = lax.all_gather(grad_output, 'head', axis=1, tiled=True)  10.3 us
    unnamed x31, local copies, waits for them, and re-layouts  6.98 us
    ppermute x2, starting transfers between devices, with_halo(): lax.ppermute(lax.slice_in_dim(block, block.shape[dim] - width, None, axis...  6.47 us
    ppermute x2, starting transfers between devices, with_halo(): lax.ppermute(lax.slice_in_dim(block, 0, width, axis=dim), axis, backward)  6.24 us
    ppermute x2, waiting for transfers between devices, with_halo(): lax.ppermute(lax.slice_in_dim(block, 0, width, axis=dim), axis, backward)  6.05 us
    another operation x3, local copies, waits for them, and re-layouts, shards(): jnp.stack([key_window, value_window]).reshape(2, 3 * tok_rows, features)  5.98 us
    dot_general x1, matrix products, key_side(): jnp.einsum('nhisj,nihd->nsjhd', prob_half, grad_sel, preferred_element_ty...  5.04 us
  transfers between devices with their start and end apart: 6, of which 3 were waited for; matrix products, arithmetic and copies ran while one was open for 33% of the time, Pallas kernels for 35%

profile of v1, /device:TPU:4, one launch (start us, length us, event | category | flops | bytes accessed | tf_op | source)
XLA Modules:
  0.0 165.4 jit_solution(13071450632953151147)
XLA Ops:
  8.4 2.4 %collective-permute-start.1 = (bf16[2,512,256]{2,1,0:T(8,128)(2,1)S(1)}, bf16[2,512,256]{2,1,0:T(8,128)(2,1)S(1)}, u32[]{:S(2)}, u32[]{:S(2)}) collective-permute-start(bf16[2,512,256]{2,1,0:T(8,128)(2,1)S(1)} %pad_maximum_fusion.4), channel_id=1, source_target_pairs={{4,0},{8,4},{12,8},{16,12},{20,16},{24,20},{28,24},{32,28},{36,32}... | collective-permute-start | bytes 1572872 | tf_op jit(solution)/shard_map/ppermute | solution.py:149
  10.8 3.4 %collective-permute-start = (bf16[2,512,256]{2,1,0:T(8,128)(2,1)S(1)}, bf16[2,512,256]{2,1,0:T(8,128)(2,1)S(1)}, u32[]{:S(2)}, u32[]{:S(2)}) collective-permute-start(bf16[2,512,256]{2,1,0:T(8,128)(2,1)S(1)} %pad_maximum_fusion.4), channel_id=1, source_target_pairs={{0,4},{4,8},{8,12},{12,16},{16,20},{20,24},{24,28},{28,32},{32,36}... | collective-permute-start | bytes 1572872 | tf_op jit(solution)/shard_map/ppermute | solution.py:146
  16.1 1.7 %reshape.68 = bf16[4,128,2,128]{3,2,1,0:T(2,128)(2,1)} reshape(bf16[512,256]{1,0:T(8,128)(2,1)} %param.7) | data formatting | bytes 524288 | tf_op jit(solution)/shard_map/reshape | solution.py:210
  17.9 6.0 %collective-permute-done.1 = bf16[2,512,256]{2,1,0:T(8,128)(2,1)S(1)} collective-permute-done((bf16[2,512,256]{2,1,0:T(8,128)(2,1)S(1)}, bf16[2,512,256]{2,1,0:T(8,128)(2,1)S(1)}, u32[]{:S(2)}, u32[]{:S(2)}) %collective-permute-start.1) | collective-permute-done | bytes 524320 | tf_op jit(solution)/shard_map/ppermute | solution.py:149
  23.9 2.2 %collective-permute-done = bf16[2,512,256]{2,1,0:T(8,128)(2,1)S(1)} collective-permute-done((bf16[2,512,256]{2,1,0:T(8,128)(2,1)S(1)}, bf16[2,512,256]{2,1,0:T(8,128)(2,1)S(1)}, u32[]{:S(2)}, u32[]{:S(2)}) %collective-permute-start) | collective-permute-done | bytes 524320 | tf_op jit(solution)/shard_map/ppermute | solution.py:146
  28.6 2.0 %squeeze.5 = bf16[12,128,2,128]{3,2,1,0:T(2,128)(2,1)S(1)} reshape(bf16[1,1536,256]{2,1,0:T(8,128)(2,1)} %get-tuple-element.10) | data formatting | bytes 1572864 | tf_op jit(solution)/shard_map/squeeze | solution.py:211
  30.7 2.2 %gather_fusion.1 = bf16[32,128,2,128]{3,1,2,0:T(8,128)(2,1)} fusion(bf16[12,128,2,128]{3,1,2,0:T(8,128)(2,1)S(1)} %copy.78, s32[1024]{0:T(1024)S(1)} %pad_clamp_fusion), kind=kCustom, calls=%fused_computation.1 | custom fusion | bytes 4194432 | tf_op jit(solution)/shard_map/gather | solution.py:211
  33.0 2.1 %gather_fusion = bf16[32,128,2,128]{3,1,2,0:T(8,128)(2,1)} fusion(bf16[12,128,2,128]{3,1,2,0:T(8,128)(2,1)S(1)} %copy.77, s32[1024]{0:T(1024)S(1)} %pad_clamp_fusion), kind=kCustom, calls=%fused_computation | custom fusion | bytes 4194432 | tf_op jit(solution)/shard_map/gather | solution.py:212
  35.1 1.7 %bitcast_reduce_fusion = (f32[4,2,128]{2,1,0:T(2,128)S(1)}, f32[4,2,8,128,128]{4,3,2,1,0:T(8,128)S(1)}) fusion(pred[4,8]{1,0:T(4,128)(4,1)S(1)} %iota_compare_fusion.1, bf16[4,128,2,128,1]{3,2,1,0,4:T(2,128)(2,1)} %bitcast.100, bf16[4,8,128,2,128]{4,2,3,1,0:T(8,128)(2,1)S(1)} %bitcast.97), kind=kOutput, calls=%fused_computation.8 | convolution fusion | flops 271580160 | bytes 6557728 | tf_op jit(solution)/shard_map/nihd,nsjhd->nhisj/dot_general | solution.py:156
  43.5 10.3 %all-gather.2.cloned.1.call-done = bf16[512,1024]{1,0:T(8,128)(2,1)} async-done(((bf16[512,256]{1,0:T(8,128)(2,1)}), bf16[512,1024]{1,0:T(8,128)(2,1)}) %all-gather.2.cloned.1.call-update) | async-done | bytes 1048592 | tf_op jit(solution)/shard_map/all_gather | solution.py:227
  53.8 1.7 %convert_multiply_fusion = (f32[512,256]{1,0:T(8,128)S(1)}, bf16[512,256]{1,0:T(8,128)(2,1)S(1)}) fusion(bf16[64,8,2,128]{3,2,1,0:T(2,128)(2,1)S(1)} %bitcast.94, bf16[512,1024]{1,0:T(8,128)(2,1)} %all-gather.2.cloned.1.call-done, bf16[256,1024]{1,0:T(8,128)(2,1)S(1)} %copy-done), kind=kOutput, calls=%fused_computation.44 | convolution fusion | flops 268959744 | bytes 2621440 | tf_op jit(solution)/shard_map/dot_general | solution.py:228
  56.6 5.0 %fusion.8 = f32[4,2,128,8,128]{2,3,0,1,4:T(8,128)} fusion(bf16[4,2,128,8,128]{2,4,3,1,0:T(8,128)(2,1)} %copy-done.12, bf16[4,128,2,128]{3,2,1,0:T(2,128)(2,1)S(1)} %reshape.70), kind=kOutput, calls=%fused_computation.15 | convolution fusion | flops 268435456 | bytes 6553600 | tf_op jit(solution)/shard_map/nhisj,nihd->nsjhd/dot_general | solution.py:176
  64.4 1.7 %fusion.19 = f32[12,128,2,128]{3,0,2,1:T(8,128)S(1)} fusion(f32[4,2,8,128,128]{4,2,0,1,3:T(8,128)S(1)} %fusion.10, s32[4,8]{1,0:T(4,128)S(1)} %copy.91), kind=kOutput, calls=%fused_computation.26 | convolution fusion | flops 150995328 | bytes 5767296 | tf_op jit(solution)/shard_map/nsw,nsjhd->wjhd/dot_general | solution.py:182
  66.2 2.1 %copy.94 = f32[12,128,2,128]{3,2,1,0:T(2,128)} copy(f32[12,128,2,128]{3,0,2,1:T(8,128)S(1)} %fusion.19) | data formatting | bytes 3145728 | tf_op jit(solution)/shard_map/nsw,nsjhd->wjhd/dot_general | solution.py:182
  68.3 2.5 %stack.21 = f32[1,1536,256]{2,1,0:T(8,128)S(1)} reshape(f32[12,128,2,128]{3,2,1,0:T(2,128)} %copy.94) | data formatting | bytes 3145728 | tf_op jit(solution)/shard_map/stack | solution.py:249
  70.9 3.4 %fusion.22 = f32[12,128,2,128]{3,0,2,1:T(8,128)S(1)} fusion(f32[4,2,128,8,128]{2,3,0,1,4:T(8,128)} %fusion.8, s32[4,8]{1,0:T(4,128)S(1)} %copy.91), kind=kOutput, calls=%fused_computation.27 | convolution fusion | flops 150995328 | bytes 5767296 | tf_op jit(solution)/shard_map/nsw,nsjhd->wjhd/dot_general | solution.py:183
  74.3 2.0 %copy.97 = f32[12,128,2,128]{3,2,1,0:T(2,128)} copy(f32[12,128,2,128]{3,0,2,1:T(8,128)S(1)} %fusion.22) | data formatting | bytes 3145728 | tf_op jit(solution)/shard_map/nsw,nsjhd->wjhd/dot_general | solution.py:183
  76.3 3.3 %stack.22 = f32[1,1536,256]{2,1,0:T(8,128)} reshape(f32[12,128,2,128]{3,2,1,0:T(2,128)} %copy.97) | data formatting | bytes 3145728 | tf_op jit(solution)/shard_map/stack | solution.py:249
  81.3 1.5 copy-done.3
  83.6 3.1 %collective-permute-start.2 = (bf16[2,512,256]{2,1,0:T(8,128)(2,1)S(1)}, bf16[2,512,256]{2,1,0:T(8,128)(2,1)}, u32[]{:S(2)}, u32[]{:S(2)}) collective-permute-start(bf16[2,512,256]{2,1,0:T(8,128)(2,1)S(1)} %get-tuple-element.7), channel_id=1, source_target_pairs={{0,4},{4,8},{8,12},{12,16},{16,20},{20,24},{24,28},{28,32},{32,36}... | collective-permute-start | bytes 1572872 | tf_op jit(solution)/shard_map/ppermute | solution.py:146
  86.7 3.8 %collective-permute-start.3 = (bf16[2,512,256]{2,1,0:T(8,128)(2,1)}, bf16[2,512,256]{2,1,0:T(8,128)(2,1)}, u32[]{:S(2)}, u32[]{:S(2)}) collective-permute-start(bf16[2,512,256]{2,1,0:T(8,128)(2,1)} %get-tuple-element.8), channel_id=1, source_target_pairs={{4,0},{8,4},{12,8},{16,12},{20,16},{24,20},{28,24},{32,28},{36,32}... | collective-permute-start | bytes 1572872 | tf_op jit(solution)/shard_map/ppermute | solution.py:149
  92.0 58.0 %ctx_sum.1 = f32[256,1024]{1,0:T(8,128)} custom-call(f32[256,1024]{1,0:T(8,128)} %fusion.45.part_ref), custom_call_target="tpu_custom_call" | custom-call | tf_op jit(solution)/shard_map/ctx_sum/pallas_call | solution.py:118
  150.0 3.1 %fusion.37 = bf16[4,128,2,128]{1,3,2,0:T(8,128)(2,1)} fusion(bf16[4,2,128,8,128]{2,4,3,1,0:T(8,128)(2,1)S(1)} %copy-done.8, bf16[4,8,128,2,128]{4,2,3,1,0:T(8,128)(2,1)} %bitcast.96), kind=kOutput, calls=%fused_computation.35 | convolution fusion | flops 268566528 | bytes 4456448 | tf_op jit(solution)/shard_map/nhisj,nsjhd->nihd/dot_general | solution.py:187
  155.0 1.8 %fusion.44 = bf16[2,512,256]{2,1,0:T(8,128)(2,1)S(1)} fusion(f32[2,1536,256]{2,1,0:T(8,128)} %copy-done.3, bf16[2,512,256]{2,1,0:T(8,128)(2,1)} %collective-permute-done.3, bf16[2,512,256]{2,1,0:T(8,128)(2,1)S(1)} %get-tuple-element.7, bf16[2,512,256]{2,1,0:T(8,128)(2,1)} %get-tuple-element.8, bf16[2,512,256]{2,1,0:T(8,128)(2,1)} %collective-permute-done.2), kind=kLoop, calls=%fused_computation.39 | loop fusion | flops 4980736 | bytes 3670016 | tf_op jit(solution)/shard_map/convert.1
  (68 shorter events, 23.9 us)
Async XLA Ops:
  7.2 34.9 %copy-start = (bf16[256,1024]{1,0:T(8,128)(2,1)S(1)}, bf16[256,1024]{1,0:T(8,128)(2,1)}, u32[]{:S(2)}) copy-start(bf16[256,1024]{1,0:T(8,128)(2,1)} %param.10) | copy-start | bytes 1572868
  7.2 46.6 %all-gather.2.cloned.1.call-start = ((), (), s32[]{:S(2)}) async-start(), calls=%async_computation.2 | async-start | bytes 1310720 | tf_op jit(solution)/shard_map/all_gather | solution.py:227
  8.4 15.6 %collective-permute-start.1 = (bf16[2,512,256]{2,1,0:T(8,128)(2,1)S(1)}, bf16[2,512,256]{2,1,0:T(8,128)(2,1)S(1)}, u32[]{:S(2)}, u32[]{:S(2)}) collective-permute-start(bf16[2,512,256]{2,1,0:T(8,128)(2,1)S(1)} %pad_maximum_fusion.4), channel_id=1, source_target_pairs={{4,0},{8,4},{12,8},{16,12},{20,16},{24,20},{28,24},{32,28},{36,32}... | collective-permute-start | bytes 1572872 | tf_op jit(solution)/shard_map/ppermute | solution.py:149
  10.8 15.3 %collective-permute-start = (bf16[2,512,256]{2,1,0:T(8,128)(2,1)S(1)}, bf16[2,512,256]{2,1,0:T(8,128)(2,1)S(1)}, u32[]{:S(2)}, u32[]{:S(2)}) collective-permute-start(bf16[2,512,256]{2,1,0:T(8,128)(2,1)S(1)} %pad_maximum_fusion.4), channel_id=1, source_target_pairs={{0,4},{4,8},{8,12},{12,16},{16,20},{20,24},{24,28},{28,32},{32,36}... | collective-permute-start | bytes 1572872 | tf_op jit(solution)/shard_map/ppermute | solution.py:146
  14.2 143.3 %reduce-scatter.2.cloned.1.call-start = ((), (), s32[]{:S(2)}) async-start(), calls=%async_computation.1 | async-start | bytes 1310720 | tf_op jit(solution)/shard_map/reduce_scatter | solution.py:224
  33.0 2.1 %copy-start.9 = (bf16[32,128,2,128]{3,1,2,0:T(8,128)(2,1)S(1)}, bf16[32,128,2,128]{3,1,2,0:T(8,128)(2,1)}, u32[]{:S(2)}) copy-start(bf16[32,128,2,128]{3,1,2,0:T(8,128)(2,1)} %gather_fusion.1) | copy-start | bytes 6291460
  36.8 2.0 %copy-start.1 = (f32[4,2,8,128,128]{4,3,2,1,0:T(8,128)}, f32[4,2,8,128,128]{4,3,2,1,0:T(8,128)S(1)}, u32[]{:S(2)}) copy-start(f32[4,2,8,128,128]{4,3,2,1,0:T(8,128)S(1)} %get-tuple-element.14) | copy-start | bytes 12582916
  38.8 2.3 %copy-start.10 = (bf16[32,128,2,128]{3,1,2,0:T(8,128)(2,1)S(1)}, bf16[32,128,2,128]{3,1,2,0:T(8,128)(2,1)}, u32[]{:S(2)}) copy-start(bf16[32,128,2,128]{3,1,2,0:T(8,128)(2,1)} %gather_fusion) | copy-start | bytes 6291460
  39.8 1.3 copy-start.12
  56.6 5.1 %copy-start.2 = (f32[4,2,8,128,128]{4,3,2,1,0:T(8,128)S(1)}, f32[4,2,8,128,128]{4,3,2,1,0:T(8,128)}, u32[]{:S(2)}) copy-start(f32[4,2,8,128,128]{4,3,2,1,0:T(8,128)} %copy-done.1) | copy-start | bytes 12582916
  56.6 5.1 %copy-start.11 = (bf16[32,128,2,128]{3,1,2,0:T(8,128)(2,1)S(1)}, bf16[32,128,2,128]{3,1,2,0:T(8,128)(2,1)}, u32[]{:S(2)}) copy-start(bf16[32,128,2,128]{3,1,2,0:T(8,128)(2,1)} %gather_fusion) | copy-start | bytes 6291460
  61.6 1.4 copy-start.13
  63.1 1.4 copy-start.7
  79.6 1.4 copy-start.4
  81.1 1.6 copy-start.3
  82.8 7.8 %copy-start.5 = (bf16[512,1024]{1,0:T(8,128)(2,1)S(1)}, bf16[512,1024]{1,0:T(8,128)(2,1)}, u32[]{:S(2)}) copy-start(bf16[512,1024]{1,0:T(8,128)(2,1)} %all-gather.2.cloned.1.call-done) | copy-start | bytes 3145732
  83.6 71.3 %collective-permute-start.2 = (bf16[2,512,256]{2,1,0:T(8,128)(2,1)S(1)}, bf16[2,512,256]{2,1,0:T(8,128)(2,1)}, u32[]{:S(2)}, u32[]{:S(2)}) collective-permute-start(bf16[2,512,256]{2,1,0:T(8,128)(2,1)S(1)} %get-tuple-element.7), channel_id=1, source_target_pairs={{0,4},{4,8},{8,12},{12,16},{16,20},{20,24},{24,28},{28,32},{32,36}... | collective-permute-start | bytes 1572872 | tf_op jit(solution)/shard_map/ppermute | solution.py:146
  86.7 63.3 %copy-start.8 = (bf16[4,2,128,8,128]{2,4,3,1,0:T(8,128)(2,1)S(1)}, bf16[4,2,128,8,128]{2,4,3,1,0:T(8,128)(2,1)}, u32[]{:S(2)}) copy-start(bf16[4,2,128,8,128]{2,4,3,1,0:T(8,128)(2,1)} %copy-done.7) | copy-start | bytes 6291460
  86.7 68.2 %collective-permute-start.3 = (bf16[2,512,256]{2,1,0:T(8,128)(2,1)}, bf16[2,512,256]{2,1,0:T(8,128)(2,1)}, u32[]{:S(2)}, u32[]{:S(2)}) collective-permute-start(bf16[2,512,256]{2,1,0:T(8,128)(2,1)} %get-tuple-element.8), channel_id=1, source_target_pairs={{4,0},{8,4},{12,8},{16,12},{20,16},{24,20},{28,24},{32,28},{36,32}... | collective-permute-start | bytes 1572872 | tf_op jit(solution)/shard_map/ppermute | solution.py:149
  155.0 2.6 %copy-start.6 = (f32[256,1024]{1,0:T(8,128)S(1)}, f32[256,1024]{1,0:T(8,128)}, u32[]{:S(2)}) copy-start(f32[256,1024]{1,0:T(8,128)} %ctx_sum.1) | copy-start | bytes 3145732
Sparse Core Ops, SparseCore 0:
  14.4 39.3 all-gather.1
  57.4 47.0 reduce-scatter.1

commit v2 on v0

v2 whole, which is shorter than its diff:
```python
import jax
import jax.numpy as jnp
from jax import lax
from jax.experimental import pallas as pl
from jax.experimental.pallas import tpu as pltpu
from jax.sharding import PartitionSpec as P

HD = 128
BLK = 128
MESH = pl.DeviceIdType.MESH
BF = jnp.bfloat16
F32 = jnp.float32
NY, NZ, NX = 4, 8, 4
NCTX = NY * NZ * NX
LOG2E = 1.4426950408889634
HEADS_HERE = 2
ROWS = 512
WINDOW = 3 * ROWS
CHUNK = 256


def dot(a, b, ca, cb):
    return lax.dot_general(a, b, (((ca,), (cb,)), ((), ())), preferred_element_type=F32)


def span(i, n):
    return pl.ds(pl.multiple_of(i * n, n), n)


def layer_kernel(
    q_ref, k_ref, v_ref, w_ref, g_ref, lists_ref, counts_ref,
    out_ref, dq_ref, dk_ref, dv_ref, dw_ref,
    kw, vw, bias, st, pt, dst, attn, ga, gfull,
    rs_send, rs_recv, rs_keep, rs2_send, rs2_recv,
    ret_send, ret_recv, own_grad,
    part32, part, xr, s1, zr, s2, yr, gy, gz, gx,
    halo_sem, head_sem, rs_sem, ret_sem, sx, sz, sy, ty, tz, tx,
):
    pos = lax.axis_index("ctx")
    hi = lax.axis_index("head")
    x = pos % NX
    z = (pos // NX) % NZ
    y = pos // (NX * NZ)
    core = hi % 2
    far = hi // 2

    def at(ctx, head):
        return {"ctx": ctx, "head": head}

    right = at((pos + 1) % NCTX, hi)
    left = at((pos + NCTX - 1) % NCTX, hi)
    mate = far * 2 + (1 - core)
    twin = (1 - far) * 2 + core
    mate_twin = (1 - far) * 2 + (1 - core)
    to_mate, to_twin = at(pos, mate), at(pos, twin)

    def x_peer(d):
        p = (x + d) % NX
        return p, at((y * NZ + z) * NX + p, hi)

    def z_peer(d):
        p = (z + d) % NZ
        return p, at((y * NZ + p) * NX + x, hi)

    def y_peer(d):
        p = (y + d) % NY
        return p, at((p * NZ + z) * NX + x, hi)

    started = []

    def send(src, dst_, sems, k, device):
        c = pltpu.make_async_remote_copy(
            src_ref=src, dst_ref=dst_, send_sem=sems.at[0, k], recv_sem=sems.at[1, k],
            device_id=device, device_id_type=MESH,
        )
        c.start()
        started.append(c)
        return c

    barrier = pltpu.get_barrier_semaphore()
    peers = [right, left, to_mate, to_twin]
    peers += [x_peer(d)[1] for d in range(1, NX)]
    peers += [z_peer(d)[1] for d in range(1, NZ)]
    peers += [y_peer(d)[1] for d in range(1, NY)]
    for device in peers:
        pl.semaphore_signal(barrier, inc=1, device_id=device, device_id_type=MESH)

    slot = lax.broadcasted_iota(jnp.int32, (1, 8), 1)
    for n in range(4):
        row = lists_ref[pl.ds(pos * 4 + n, 1), :]
        used = slot < counts_ref[pos * 4 + n]
        for wb in range(12):
            block = ((pos + NCTX - 1) * 4 + wb) % (NCTX * 4)
            hit = jnp.where(used & (row == block), 1.0, 0.0)
            hit = jnp.max(hit, axis=1, keepdims=True)
            value = jnp.where(hit > 0.5, 0.0, -jnp.inf)
            bias[wb : wb + 1, n * BLK : (n + 1) * BLK] = jnp.broadcast_to(value, (1, BLK))
    kw[ROWS : 2 * ROWS] = k_ref[...]
    vw[ROWS : 2 * ROWS] = v_ref[...]
    gfull[:, span(hi, 256)] = g_ref[...]
    pl.semaphore_wait(barrier, len(peers))

    halo = [
        send(k_ref, kw.at[0:ROWS], halo_sem, 0, right),
        send(k_ref, kw.at[2 * ROWS : 3 * ROWS], halo_sem, 1, left),
    ]
    g_twin = send(g_ref, gfull.at[:, span(hi, 256)], head_sem, 0, to_twin)
    halo += [
        send(v_ref, vw.at[0:ROWS], halo_sem, 2, right),
        send(v_ref, vw.at[2 * ROWS : 3 * ROWS], halo_sem, 3, left),
    ]
    g_mate = send(g_ref, gfull.at[:, span(hi, 256)], head_sem, 1, to_mate)

    factor = HD ** (-0.5)

    def score_chunk(h, c):
        hc = slice(h * HD, (h + 1) * HD)
        s = dot(kw[c * CHUNK : (c + 1) * CHUNK, hc], q_ref[:, hc], 1, 1) * (factor * LOG2E)
        for b in range(CHUNK // BLK):
            wb = c * (CHUNK // BLK) + b
            st[h, wb * BLK : (wb + 1) * BLK] = s[b * BLK : (b + 1) * BLK] + bias[wb : wb + 1]

    for h in range(HEADS_HERE):
        for c in (2, 3):
            score_chunk(h, c)
    halo[0].wait_recv()
    for h in range(HEADS_HERE):
        for c in (0, 1):
            score_chunk(h, c)
    halo[1].wait_recv()
    for h in range(HEADS_HERE):
        for c in (4, 5):
            score_chunk(h, c)
    for h in range(HEADS_HERE):
        top = jnp.max(st[h], axis=0, keepdims=True)
        total = jnp.zeros((1, ROWS), F32)
        for c in range(WINDOW // CHUNK):
            keys = slice(c * CHUNK, (c + 1) * CHUNK)
            e = jnp.exp2(st[h, keys] - top)
            st[h, keys] = e
            total = total + jnp.sum(e, axis=0, keepdims=True)
        inverse = 1.0 / total
        for c in range(WINDOW // CHUNK):
            keys = slice(c * CHUNK, (c + 1) * CHUNK)
            pt[h, keys] = (st[h, keys] * inverse).astype(BF)
    halo[2].wait_recv()
    halo[3].wait_recv()
    attn_t = []
    for h in range(HEADS_HERE):
        hc = slice(h * HD, (h + 1) * HD)
        mixed = dot(vw[:, hc], pt[h], 0, 0)
        attn_t.append(mixed.astype(BF))
        attn[:, hc] = jnp.transpose(mixed).astype(BF)

    g_twin.wait_recv()
    g_relay = send(
        gfull.at[:, span(twin, 256)], gfull.at[:, span(twin, 256)], head_sem, 2, to_mate
    )
    for f in range(2):
        cols = span(f * 2 + (1 - core), 256)
        rs_send[f] = dot(attn[...], w_ref[:, cols], 1, 0).astype(BF)
    rs = [send(rs_send.at[f], rs_recv.at[f], rs_sem, f, to_mate) for f in range(2)]
    for f in range(2):
        cols = span(f * 2 + core, 256)
        rs_keep[f] = dot(attn[...], w_ref[:, cols], 1, 0)
    g_mate.wait_recv()
    g_relay.wait_recv()

    for h in range(HEADS_HERE):
        value = dot(attn_t[h], gfull[...], 1, 0)
        part32[h * HD : (h + 1) * HD] = value
        part[h * HD : (h + 1) * HD] = value.astype(BF)
    xs = []
    for d in range(1, NX):
        p, device = x_peer(d)
        xs.append(send(part.at[span(p, 64)], xr.at[d - 1], sx, d - 1, device))

    row_dots = []
    for h in range(HEADS_HERE):
        hc = slice(h * HD, (h + 1) * HD)
        back = dot(w_ref[hc], gfull[...], 1, 1).astype(BF).astype(F32)
        row_dots.append(jnp.sum(back * attn_t[h].astype(F32), axis=0, keepdims=True))
        ga[:, hc] = jnp.transpose(back).astype(BF)

    for c in rs:
        c.wait_recv()
    rs2_send[...] = (rs_keep[1 - far] + rs_recv[1 - far].astype(F32)).astype(BF)
    rs2 = send(rs2_send, rs2_recv, rs_sem, 2, to_twin)

    def back_chunk(h, c):
        hc = slice(h * HD, (h + 1) * HD)
        keys = slice(c * CHUNK, (c + 1) * CHUNK)
        dp = dot(vw[keys, hc], ga[:, hc], 1, 1)
        ds = pt[h, keys].astype(F32) * ((dp - row_dots[h]) * factor)
        dst[h, keys] = ds.astype(BF)

    def key_grads(h, side):
        hc = slice(h * HD, (h + 1) * HD)
        keys = slice(side * ROWS, (side + 1) * ROWS)
        return dot(dst[h, keys], q_ref[:, hc], 1, 0), dot(pt[h, keys], ga[:, hc], 1, 0)

    rets = []
    for i, side, device in ((0, 2, right), (1, 0, left)):
        for h in range(HEADS_HERE):
            hc = slice(h * HD, (h + 1) * HD)
            for c in (side * 2, side * 2 + 1):
                back_chunk(h, c)
            dk, dv = key_grads(h, side)
            ret_send[i, 0, :, hc] = dk.astype(BF)
            ret_send[i, 1, :, hc] = dv.astype(BF)
        rets.append(send(ret_send.at[i], ret_recv.at[i], ret_sem, i, device))

    for c in xs:
        c.wait_recv()
    total = part32[span(x, 64)]
    for d in range(NX - 1):
        total = total + xr[d].astype(F32)
    s1[...] = total.astype(BF)
    zs = []
    for d in range(1, NZ):
        p, device = z_peer(d)
        zs.append(send(s1.at[:, span(p, 128)], zr.at[d - 1], sz, d - 1, device))

    for h in range(HEADS_HERE):
        hc = slice(h * HD, (h + 1) * HD)
        for c in (2, 3):
            back_chunk(h, c)
        dk, dv = key_grads(h, 1)
        own_grad[0, :, hc] = dk
        own_grad[1, :, hc] = dv

    for c in zs:
        c.wait_recv()
    total = s1[:, span(z, 128)].astype(F32)
    for d in range(NZ - 1):
        total = total + zr[d].astype(F32)
    s2[...] = total.astype(BF)
    ys = []
    for d in range(1, NY):
        p, device = y_peer(d)
        ys.append(send(s2.at[span(p, 16)], yr.at[d - 1], sy, d - 1, device))

    for h in range(HEADS_HERE):
        hc = slice(h * HD, (h + 1) * HD)
        grad = dot(kw[:, hc], dst[h], 0, 0)
        dq_ref[:, hc] = jnp.transpose(grad).astype(BF)

    for c in ys:
        c.wait_recv()
    total = s2[span(y, 16)].astype(F32)
    for d in range(NY - 1):
        total = total + yr[d].astype(F32)
    gy[span(y, 16)] = total.astype(BF)
    ys = []
    for d in range(1, NY):
        ys.append(send(gy.at[span(y, 16)], gy.at[span(y, 16)], ty, d - 1, y_peer(d)[1]))
    for c in ys:
        c.wait_recv()
    zs = []
    for d in range(1, NZ):
        zs.append(send(gy, gz.at[:, span(z, 128)], tz, d - 1, z_peer(d)[1]))
    gz[:, span(z, 128)] = gy[...]
    for c in zs:
        c.wait_recv()
    xs = []
    for d in range(1, NX):
        xs.append(send(gz, gx.at[span(x, 64)], tx, d - 1, x_peer(d)[1]))
    gx[span(x, 64)] = gz[...]

    rs2.wait_recv()
    out_ref[...] = (
        rs_keep[far] + rs_recv[far].astype(F32) + rs2_recv[...].astype(F32)
    ).astype(BF)
    for c in rets:
        c.wait_recv()
    for i, ref in ((0, dk_ref), (1, dv_ref)):
        ref[...] = (
            own_grad[i] + ret_recv[0, i].astype(F32) + ret_recv[1, i].astype(F32)
        ).astype(BF)
    for c in xs:
        c.wait_recv()
    dw_ref[...] = gx[...].astype(F32) * (NCTX * ROWS) ** (-0.5)
    for c in started:
        c.wait_send()


def shards(queries, keys, values, out_weight, grad_output, key_lists, key_counts):
    vmem = pl.BlockSpec(memory_space=pltpu.VMEM)
    smem = pl.BlockSpec(memory_space=pltpu.SMEM)
    dma = lambda n: pltpu.SemaphoreType.DMA((2, n))
    tok = jax.ShapeDtypeStruct(queries.shape, BF)
    return pl.pallas_call(
        layer_kernel,
        out_shape=(tok, tok, tok, tok, jax.ShapeDtypeStruct(out_weight.shape, F32)),
        in_specs=[vmem] * 6 + [smem],
        out_specs=[vmem] * 5,
        scratch_shapes=[
            pltpu.VMEM((WINDOW, 256), BF),
            pltpu.VMEM((WINDOW, 256), BF),
            pltpu.VMEM((16, ROWS), F32),
            pltpu.VMEM((HEADS_HERE, WINDOW, ROWS), F32),
            pltpu.VMEM((HEADS_HERE, WINDOW, ROWS), BF),
            pltpu.VMEM((HEADS_HERE, WINDOW, ROWS), BF),
            pltpu.VMEM((ROWS, 256), BF),
            pltpu.VMEM((ROWS, 256), BF),
            pltpu.VMEM((ROWS, 1024), BF),
            pltpu.VMEM((2, ROWS, 256), BF),
            pltpu.VMEM((2, ROWS, 256), BF),
            pltpu.VMEM((2, ROWS, 256), F32),
            pltpu.VMEM((ROWS, 256), BF),
            pltpu.VMEM((ROWS, 256), BF),
            pltpu.VMEM((2, 2, ROWS, 256), BF),
            pltpu.VMEM((2, 2, ROWS, 256), BF),
            pltpu.VMEM((2, ROWS, 256), F32),
            pltpu.VMEM((256, 1024), F32),
            pltpu.VMEM((256, 1024), BF),
            pltpu.VMEM((NX - 1, 64, 1024), BF),
            pltpu.VMEM((64, 1024), BF),
            pltpu.VMEM((NZ - 1, 64, 128), BF),
            pltpu.VMEM((64, 128), BF),
            pltpu.VMEM((NY - 1, 16, 128), BF),
            pltpu.VMEM((64, 128), BF),
            pltpu.VMEM((64, 1024), BF),
            pltpu.VMEM((256, 1024), BF),
            dma(4), dma(3), dma(3), dma(2),
            dma(NX - 1), dma(NZ - 1), dma(NY - 1), dma(NY - 1), dma(NZ - 1), dma(NX - 1),
        ],
        compiler_params=pltpu.CompilerParams(
            collective_id=0, has_side_effects=True, vmem_limit_bytes=62 * 1024 * 1024
        ),
        name="layer",
    )(queries, keys, values, out_weight, grad_output, key_lists, key_counts)


def solution(mesh):
    in_specs = (
        P("ctx", "head"),
        P("ctx", "head"),
        P("ctx", "head"),
        P("head", None),
        P("ctx", "head"),
        P(),
        P(),
    )
    out_specs = (
        P("ctx", "head"),
        P("ctx", "head"),
        P("ctx", "head"),
        P("ctx", "head"),
        P("head", None),
    )
    return jax.shard_map(shards, mesh=mesh, in_specs=in_specs, out_specs=out_specs, check_vma=False)
```

time: 1520 us -> 96.6 us (0.06)
  the two profiles are of different devices: /device:TPU:1 before, /device:TPU:68 now
where the time goes in v2:
time: 96.6 us; the launch traced here: 96.4 us
  Pallas kernels  88.3 us (91%)
  local copies, waits for them, and re-layouts  7.42 us (8%)
    pallas_call x1, Pallas kernels, shards(): pl.pallas_call(layer_kernel, out_shape=(tok, tok, tok, tok, jax.ShapeDtyp...  88.3 us
    unnamed x12, local copies, waits for them, and re-layouts  7.42 us

profile of v2, /device:TPU:68, one launch (start us, length us, event | category | flops | bytes accessed | tf_op | source)
XLA Modules:
  0.0 96.4 jit_solution(15671823457216545623)
XLA Ops:
  0.6 1.6 %copy.12.lists_ref = s32[512,8]{1,0:T(8,128)} copy(s32[512,8]{0,1:T(8,128)} %param.12) | data formatting | bytes 32768 | tf_op args[5]
  2.2 88.3 %layer.1 = (bf16[512,256]{1,0:T(8,128)(2,1)}, bf16[512,256]{1,0:T(8,128)(2,1)}, bf16[512,256]{1,0:T(8,128)(2,1)}, bf16[512,256]{1,0:T(8,128)(2,1)}, f32[256,1024]{1,0:T(8,128)}) custom-call(bf16[512,256]{1,0:T(8,128)(2,1)} %q_ref.1, bf16[512,256]{1,0:T(8,128)(2,1)} %k_ref.1, bf16[512,256]{1,0:T(8,128)(2,1)} %v_ref.1, bf16[256,1024]{1,0:T(8,128)(2,1)} %w_ref.1, ...), custom_call_target="tpu_custom_call" | custom-call | tf_op jit(solution)/shard_map/layer/pallas_call | solution.py:292
  90.5 0.0 copy-start.2
  90.5 0.0 copy-start
  90.5 1.8 %copy.18 = bf16[512,256]{1,0:T(8,128)(2,1)} copy(bf16[512,256]{1,0:T(8,128)(2,1)} %get-tuple-element.10) | data formatting | bytes 524288
  92.3 0.0 copy-done.2
  92.3 0.7 copy.19
  93.0 0.0 copy-start.1
  93.0 1.7 %copy.20 = bf16[512,256]{1,0:T(8,128)(2,1)} copy(bf16[512,256]{1,0:T(8,128)(2,1)} %get-tuple-element.12) | data formatting | bytes 524288
  94.7 0.0 copy-done.1
  94.7 0.7 copy.21
  95.4 0.0 copy-done
  95.4 1.0 %copy.22 = f32[256,1024]{1,0:T(8,128)} copy(f32[256,1024]{1,0:T(8,128)S(1)} %copy-done) | data formatting | bytes 2097152
Async XLA Ops:
  90.5 1.8 %copy-start.2 = (bf16[512,256]{1,0:T(8,128)(2,1)S(1)}, bf16[512,256]{1,0:T(8,128)(2,1)}, u32[]{:S(2)}) copy-start(bf16[512,256]{1,0:T(8,128)(2,1)} %get-tuple-element.11) | copy-start | bytes 786436
  90.5 4.9 %copy-start = (f32[256,1024]{1,0:T(8,128)S(1)}, f32[256,1024]{1,0:T(8,128)}, u32[]{:S(2)}) copy-start(f32[256,1024]{1,0:T(8,128)} %get-tuple-element.14) | copy-start | bytes 3145732
  93.0 1.7 %copy-start.1 = (bf16[512,256]{1,0:T(8,128)(2,1)S(1)}, bf16[512,256]{1,0:T(8,128)(2,1)}, u32[]{:S(2)}) copy-start(bf16[512,256]{1,0:T(8,128)(2,1)} %get-tuple-element.13) | copy-start | bytes 786436

commit v3 on v2

--- a/solution.py
+++ b/solution.py
@@ -32,9 +32,10 @@
     out_ref, dq_ref, dk_ref, dv_ref, dw_ref,
     kw, vw, bias, st, pt, dst, attn, ga, gfull,
     rs_send, rs_recv, rs_keep, rs2_send, rs2_recv,
-    ret_send, ret_recv, own_grad,
-    part32, part, xr, s1, zr, s2, yr, gy, gz, gx,
-    halo_sem, head_sem, rs_sem, ret_sem, sx, sz, sy, ty, tz, tx,
+    ret_send, ret_recv, own_grad, relay, relay2,
+    part32, part, ax, as1, az, ay, agz, agx, bz, bs1, bx, by, bgx, bgz,
+    halo_sem, head_sem, rs_sem, ret_sem, hop_sem, hop2_sem,
+    sax, saz, say, taz, tax, sbz, sbx, sby, tbx, tbz,
 ):
     pos = lax.axis_index("ctx")
     hi = lax.axis_index("head")
@@ -51,8 +52,14 @@
     left = at((pos + NCTX - 1) % NCTX, hi)
     mate = far * 2 + (1 - core)
     twin = (1 - far) * 2 + core
-    mate_twin = (1 - far) * 2 + (1 - core)
-    to_mate, to_twin = at(pos, mate), at(pos, twin)
+    to_mate = at(pos, mate)
+
+    def y_hop(d):
+        p = (far * NY + y + d) % (2 * NY)
+        head = (p // NY) * 2 + core
+        return head, at(((p % NY) * NZ + z) * NX + x, head)
+
+    (up_head, up), (down_head, down) = y_hop(2), y_hop(6)
 
     def x_peer(d):
         p = (x + d) % NX
@@ -78,23 +85,13 @@
         return c
 
     barrier = pltpu.get_barrier_semaphore()
-    peers = [right, left, to_mate, to_twin]
+    peers = [right, left, to_mate, up, down]
     peers += [x_peer(d)[1] for d in range(1, NX)]
     peers += [z_peer(d)[1] for d in range(1, NZ)]
     peers += [y_peer(d)[1] for d in range(1, NY)]
     for device in peers:
         pl.semaphore_signal(barrier, inc=1, device_id=device, device_id_type=MESH)
 
-    slot = lax.broadcasted_iota(jnp.int32, (1, 8), 1)
-    for n in range(4):
-        row = lists_ref[pl.ds(pos * 4 + n, 1), :]
-        used = slot < counts_ref[pos * 4 + n]
-        for wb in range(12):
-            block = ((pos + NCTX - 1) * 4 + wb) % (NCTX * 4)
-            hit = jnp.where(used & (row == block), 1.0, 0.0)
-            hit = jnp.max(hit, axis=1, keepdims=True)
-            value = jnp.where(hit > 0.5, 0.0, -jnp.inf)
-            bias[wb : wb + 1, n * BLK : (n + 1) * BLK] = jnp.broadcast_to(value, (1, BLK))
     kw[ROWS : 2 * ROWS] = k_ref[...]
     vw[ROWS : 2 * ROWS] = v_ref[...]
     gfull[:, span(hi, 256)] = g_ref[...]
@@ -104,13 +101,41 @@
         send(k_ref, kw.at[0:ROWS], halo_sem, 0, right),
         send(k_ref, kw.at[2 * ROWS : 3 * ROWS], halo_sem, 1, left),
     ]
-    g_twin = send(g_ref, gfull.at[:, span(hi, 256)], head_sem, 0, to_twin)
+    quarter = lambda c: slice(c * BLK, (c + 1) * BLK)
+    hops = [None] * 4
+    for c in (0, 2, 1, 3):
+        device = up if c < 2 else down
+        hops[c] = send(g_ref.at[quarter(c)], relay.at[c], hop_sem, c, device)
     halo += [
         send(v_ref, vw.at[0:ROWS], halo_sem, 2, right),
         send(v_ref, vw.at[2 * ROWS : 3 * ROWS], halo_sem, 3, left),
     ]
     g_mate = send(g_ref, gfull.at[:, span(hi, 256)], head_sem, 1, to_mate)
 
+    g_far = []
+    rs2 = []
+
+    def pass_on(c):
+        hops[c].wait_recv()
+        device, head = (up, down_head) if c < 2 else (down, up_head)
+        g_far.append(
+            send(relay.at[c], gfull.at[quarter(c), span(head, 256)], hop_sem, 4 + c, device)
+        )
+
+    tile = lists_ref[:, span(pos // 32, 128)].astype(F32)
+    slot = lax.broadcasted_iota(jnp.int32, (8, BLK), 0)
+    lane = lax.broadcasted_iota(jnp.int32, (8, BLK), 1)
+    for n in range(4):
+        row = jnp.max(
+            jnp.where(lane == (pos % 32) * 4 + n, tile, -1.0), axis=1, keepdims=True
+        )
+        row = jnp.where(slot < counts_ref[pos * 4 + n], jnp.broadcast_to(row, (8, BLK)), -1.0)
+        for wb in range(12):
+            block = ((pos + NCTX - 1) * 4 + wb) % (NCTX * 4)
+            hit = jnp.where(row == block.astype(F32), 1.0, 0.0)
+            hit = jnp.max(hit, axis=0, keepdims=True)
+            bias[wb : wb + 1, n * BLK : (n + 1) * BLK] = jnp.where(hit > 0.5, 0.0, -jnp.inf)
+
     factor = HD ** (-0.5)
 
     def score_chunk(h, c):
@@ -123,10 +148,14 @@
     for h in range(HEADS_HERE):
         for c in (2, 3):
             score_chunk(h, c)
+    pass_on(0)
+    pass_on(2)
     halo[0].wait_recv()
     for h in range(HEADS_HERE):
         for c in (0, 1):
             score_chunk(h, c)
+    pass_on(1)
+    pass_on(3)
     halo[1].wait_recv()
     for h in range(HEADS_HERE):
         for c in (4, 5):
@@ -152,10 +181,11 @@
         attn_t.append(mixed.astype(BF))
         attn[:, hc] = jnp.transpose(mixed).astype(BF)
 
-    g_twin.wait_recv()
-    g_relay = send(
-        gfull.at[:, span(twin, 256)], gfull.at[:, span(twin, 256)], head_sem, 2, to_mate
-    )
+    g_share = []
+    for c, got in zip((0, 2, 1, 3), g_far):
+        got.wait_recv()
+        view = gfull.at[quarter(c), span(twin, 256)]
+        g_share.append(send(view, view, head_sem, 2 + c, to_mate))
     for f in range(2):
         cols = span(f * 2 + (1 - core), 256)
         rs_send[f] = dot(attn[...], w_ref[:, cols], 1, 0).astype(BF)
@@ -164,16 +194,21 @@
         cols = span(f * 2 + core, 256)
         rs_keep[f] = dot(attn[...], w_ref[:, cols], 1, 0)
     g_mate.wait_recv()
-    g_relay.wait_recv()
+    for c in g_share:
+        c.wait_recv()
 
     for h in range(HEADS_HERE):
         value = dot(attn_t[h], gfull[...], 1, 0)
         part32[h * HD : (h + 1) * HD] = value
         part[h * HD : (h + 1) * HD] = value.astype(BF)
-    xs = []
+    cut = 4 * HD
+    a_x, b_z = [], []
     for d in range(1, NX):
         p, device = x_peer(d)
-        xs.append(send(part.at[span(p, 64)], xr.at[d - 1], sx, d - 1, device))
+        a_x.append(send(part.at[:, span(p, 128)], ax.at[d - 1], sax, d - 1, device))
+    for d in range(1, NZ):
+        p, device = z_peer(d)
+        b_z.append(send(part.at[span(p, 32), cut:], bz.at[d - 1], sbz, d - 1, device))
 
     row_dots = []
     for h in range(HEADS_HERE):
@@ -185,7 +220,16 @@
     for c in rs:
         c.wait_recv()
     rs2_send[...] = (rs_keep[1 - far] + rs_recv[1 - far].astype(F32)).astype(BF)
-    rs2 = send(rs2_send, rs2_recv, rs_sem, 2, to_twin)
+    hops2 = [None] * 4
+    for c in (0, 2, 1, 3):
+        device = up if c < 2 else down
+        hops2[c] = send(rs2_send.at[quarter(c)], relay2.at[c], hop2_sem, c, device)
+
+    def pass_on2(c):
+        hops2[c].wait_recv()
+        rs2.append(
+            send(relay2.at[c], rs2_recv.at[quarter(c)], hop2_sem, 4 + c, up if c < 2 else down)
+        )
 
     def back_chunk(h, c):
         hc = slice(h * HD, (h + 1) * HD)
@@ -210,16 +254,25 @@
             ret_send[i, 1, :, hc] = dv.astype(BF)
         rets.append(send(ret_send.at[i], ret_recv.at[i], ret_sem, i, device))
 
-    for c in xs:
-        c.wait_recv()
-    total = part32[span(x, 64)]
-    for d in range(NX - 1):
-        total = total + xr[d].astype(F32)
-    s1[...] = total.astype(BF)
-    zs = []
+    def total_of(first, copies, slots):
+        value = first.astype(F32)
+        for i, c in enumerate(copies):
+            c.wait_recv()
+            value = value + slots[i].astype(F32)
+        return value.astype(BF)
+
+    as1[...] = total_of(part32[:, span(x, 128)], a_x, ax)
+    a_z = []
     for d in range(1, NZ):
         p, device = z_peer(d)
-        zs.append(send(s1.at[:, span(p, 128)], zr.at[d - 1], sz, d - 1, device))
+        a_z.append(send(as1.at[span(p, 32)], az.at[d - 1], saz, d - 1, device))
+    bs1[...] = total_of(part32[span(z, 32), cut:], b_z, bz)
+    b_x = []
+    for d in range(1, NX):
+        p, device = x_peer(d)
+        b_x.append(send(bs1.at[:, span(p, 128)], bx.at[d - 1], sbx, d - 1, device))
+    pass_on2(0)
+    pass_on2(2)
 
     for h in range(HEADS_HERE):
         hc = slice(h * HD, (h + 1) * HD)
@@ -229,45 +282,43 @@
         own_grad[0, :, hc] = dk
         own_grad[1, :, hc] = dv
 
-    for c in zs:
-        c.wait_recv()
-    total = s1[:, span(z, 128)].astype(F32)
-    for d in range(NZ - 1):
-        total = total + zr[d].astype(F32)
-    s2[...] = total.astype(BF)
-    ys = []
-    for d in range(1, NY):
-        p, device = y_peer(d)
-        ys.append(send(s2.at[span(p, 16)], yr.at[d - 1], sy, d - 1, device))
+    ay[y] = total_of(as1[span(z, 32)], a_z, az)
+    a_y = [send(ay.at[y], ay.at[y], say, d - 1, y_peer(d)[1]) for d in range(1, NY)]
+    by[y] = total_of(bs1[:, span(x, 128)], b_x, bx)
+    b_y = [send(by.at[y], by.at[y], sby, d - 1, y_peer(d)[1]) for d in range(1, NY)]
+    pass_on2(1)
+    pass_on2(3)
 
     for h in range(HEADS_HERE):
         hc = slice(h * HD, (h + 1) * HD)
         grad = dot(kw[:, hc], dst[h], 0, 0)
         dq_ref[:, hc] = jnp.transpose(grad).astype(BF)
 
-    for c in ys:
-        c.wait_recv()
-    total = s2[span(y, 16)].astype(F32)
-    for d in range(NY - 1):
-        total = total + yr[d].astype(F32)
-    gy[span(y, 16)] = total.astype(BF)
-    ys = []
-    for d in range(1, NY):
-        ys.append(send(gy.at[span(y, 16)], gy.at[span(y, 16)], ty, d - 1, y_peer(d)[1]))
-    for c in ys:
-        c.wait_recv()
-    zs = []
-    for d in range(1, NZ):
-        zs.append(send(gy, gz.at[:, span(z, 128)], tz, d - 1, z_peer(d)[1]))
-    gz[:, span(z, 128)] = gy[...]
-    for c in zs:
-        c.wait_recv()
-    xs = []
-    for d in range(1, NX):
-        xs.append(send(gz, gx.at[span(x, 64)], tx, d - 1, x_peer(d)[1]))
-    gx[span(x, 64)] = gz[...]
-
-    rs2.wait_recv()
+    def y_total(copies, slots):
+        for c in copies:
+            c.wait_recv()
+        value = slots[0].astype(F32)
+        for i in range(1, NY):
+            value = value + slots[i].astype(F32)
+        return value.astype(BF)
+
+    agz[span(z, 32)] = y_total(a_y, ay)
+    view = agz.at[span(z, 32)]
+    a_gz = [send(view, view, taz, d - 1, z_peer(d)[1]) for d in range(1, NZ)]
+    bgx[:, span(x, 128)] = y_total(b_y, by)
+    view_b = bgx.at[:, span(x, 128)]
+    b_gx = [send(view_b, view_b, tbx, d - 1, x_peer(d)[1]) for d in range(1, NX)]
+    for c in b_gx:
+        c.wait_recv()
+    b_gz = [send(bgx, bgz.at[span(z, 32)], tbz, d - 1, z_peer(d)[1]) for d in range(1, NZ)]
+    bgz[span(z, 32)] = bgx[...]
+    for c in a_gz:
+        c.wait_recv()
+    a_gx = [send(agz, agx.at[:, span(x, 128)], tax, d - 1, x_peer(d)[1]) for d in range(1, NX)]
+    agx[:, span(x, 128)] = agz[...]
+
+    for c in rs2:
+        c.wait_recv()
     out_ref[...] = (
         rs_keep[far] + rs_recv[far].astype(F32) + rs2_recv[...].astype(F32)
     ).astype(BF)
@@ -277,11 +328,45 @@
         ref[...] = (
             own_grad[i] + ret_recv[0, i].astype(F32) + ret_recv[1, i].astype(F32)
         ).astype(BF)
-    for c in xs:
-        c.wait_recv()
-    dw_ref[...] = gx[...].astype(F32) * (NCTX * ROWS) ** (-0.5)
+    scale = (NCTX * ROWS) ** (-0.5)
+    for c in b_gz:
+        c.wait_recv()
+    dw_ref[:, cut:] = bgz[...].astype(F32) * scale
+    for c in a_gx:
+        c.wait_recv()
+    dw_ref[:, :cut] = agx[...].astype(F32) * scale
     for c in started:
         c.wait_send()
+
+
+def hand_out_kernel(*refs):
+    n = len(refs) // 3
+    sources, targets, held = refs[:n], refs[n : 2 * n], refs[2 * n : 3 * n]
+    sem = refs[3 * n]
+    reads = [pltpu.make_async_copy(sources[i], held[i], sem.at[0, i]) for i in range(n)]
+    writes = [pltpu.make_async_copy(held[i], targets[i], sem.at[1, i]) for i in range(n)]
+    for c in reads:
+        c.start()
+    for i in range(n):
+        reads[i].wait()
+        writes[i].start()
+    for c in writes:
+        c.wait()
+
+
+def hand_out(arrays):
+    shapes = [jax.ShapeDtypeStruct(a.shape, a.dtype) for a in arrays]
+    n = len(arrays)
+    hbm = pl.BlockSpec(memory_space=pl.ANY)
+    return pl.pallas_call(
+        hand_out_kernel,
+        out_shape=shapes,
+        in_specs=[hbm] * n,
+        out_specs=[hbm] * n,
+        scratch_shapes=[pltpu.VMEM(a.shape, a.dtype) for a in arrays]
+        + [pltpu.SemaphoreType.DMA((2, n))],
+        name="hand_out",
+    )(*arrays)
 
 
 def shards(queries, keys, values, out_weight, grad_output, key_lists, key_counts):
@@ -289,7 +374,7 @@
     smem = pl.BlockSpec(memory_space=pltpu.SMEM)
     dma = lambda n: pltpu.SemaphoreType.DMA((2, n))
     tok = jax.ShapeDtypeStruct(queries.shape, BF)
-    return pl.pallas_call(
+    results = pl.pallas_call(
         layer_kernel,
         out_shape=(tok, tok, tok, tok, jax.ShapeDtypeStruct(out_weight.shape, F32)),
         in_specs=[vmem] * 6 + [smem],
@@ -312,24 +397,32 @@
             pltpu.VMEM((2, 2, ROWS, 256), BF),
             pltpu.VMEM((2, 2, ROWS, 256), BF),
             pltpu.VMEM((2, ROWS, 256), F32),
+            pltpu.VMEM((4, BLK, 256), BF),
+            pltpu.VMEM((4, BLK, 256), BF),
             pltpu.VMEM((256, 1024), F32),
             pltpu.VMEM((256, 1024), BF),
-            pltpu.VMEM((NX - 1, 64, 1024), BF),
-            pltpu.VMEM((64, 1024), BF),
-            pltpu.VMEM((NZ - 1, 64, 128), BF),
-            pltpu.VMEM((64, 128), BF),
-            pltpu.VMEM((NY - 1, 16, 128), BF),
-            pltpu.VMEM((64, 128), BF),
-            pltpu.VMEM((64, 1024), BF),
-            pltpu.VMEM((256, 1024), BF),
-            dma(4), dma(3), dma(3), dma(2),
-            dma(NX - 1), dma(NZ - 1), dma(NY - 1), dma(NY - 1), dma(NZ - 1), dma(NX - 1),
+            pltpu.VMEM((NX - 1, 256, 128), BF),
+            pltpu.VMEM((256, 128), BF),
+            pltpu.VMEM((NZ - 1, 32, 128), BF),
+            pltpu.VMEM((NY, 32, 128), BF),
+            pltpu.VMEM((256, 128), BF),
+            pltpu.VMEM((256, 512), BF),
+            pltpu.VMEM((NZ - 1, 32, 512), BF),
+            pltpu.VMEM((32, 512), BF),
+            pltpu.VMEM((NX - 1, 32, 128), BF),
+            pltpu.VMEM((NY, 32, 128), BF),
+            pltpu.VMEM((32, 512), BF),
+            pltpu.VMEM((256, 512), BF),
+            dma(4), dma(6), dma(2), dma(2), dma(8), dma(8),
+            dma(NX - 1), dma(NZ - 1), dma(NY - 1), dma(NZ - 1), dma(NX - 1),
+            dma(NZ - 1), dma(NX - 1), dma(NY - 1), dma(NX - 1), dma(NZ - 1),
         ],
         compiler_params=pltpu.CompilerParams(
             collective_id=0, has_side_effects=True, vmem_limit_bytes=62 * 1024 * 1024
         ),
         name="layer",
-    )(queries, keys, values, out_weight, grad_output, key_lists, key_counts)
+    )(queries, keys, values, out_weight, grad_output, key_lists.T, key_counts)
+    return hand_out(results)
 
 
 def solution(mesh):

time: 96.6 us -> 86.5 us (0.90)
  the two profiles are of different devices: /device:TPU:68 before, /device:TPU:1 now
where the time goes in v3:
time: 86.5 us; the launch traced here: 85.4 us
  Pallas kernels  84.8 us (98%)
    pallas_call x1, Pallas kernels, shards(): pl.pallas_call(layer_kernel, out_shape=(tok, tok, tok, tok, jax.ShapeDtyp...  82.2 us
    pallas_call x1, Pallas kernels, hand_out(): pl.pallas_call(hand_out_kernel, out_shape=shapes, in_specs=[hbm] * n, out...  2.61 us

profile of v3, /device:TPU:1, one launch (start us, length us, event | category | flops | bytes accessed | tf_op | source)
XLA Modules:
  0.0 85.4 jit_solution(8476297999432162125)
XLA Ops:
  0.6 82.2 %layer.1 = (bf16[512,256]{1,0:T(8,128)(2,1)}, bf16[512,256]{1,0:T(8,128)(2,1)}, bf16[512,256]{1,0:T(8,128)(2,1)}, bf16[512,256]{1,0:T(8,128)(2,1)}, f32[256,1024]{1,0:T(8,128)}) custom-call(bf16[512,256]{1,0:T(8,128)(2,1)} %q_ref.1, bf16[512,256]{1,0:T(8,128)(2,1)} %k_ref.1, bf16[512,256]{1,0:T(8,128)(2,1)} %v_ref.1, bf16[256,1024]{1,0:T(8,128)(2,1)} %w_ref.1, ...), custom_call_target="tpu_custom_call" | custom-call | tf_op jit(solution)/shard_map/layer/pallas_call | solution.py:377
  82.8 2.6 %hand_out.1 = (bf16[512,256]{1,0:T(8,128)(2,1)}, bf16[512,256]{1,0:T(8,128)(2,1)}, bf16[512,256]{1,0:T(8,128)(2,1)}, bf16[512,256]{1,0:T(8,128)(2,1)}, f32[256,1024]{1,0:T(8,128)}) custom-call(bf16[512,256]{1,0:T(8,128)(2,1)} %get-tuple-element.10.refs_0_, bf16[512,256]{1,0:T(8,128)(2,1)} %get-tuple-element.11.refs_1_, ...), custom_call_target="tpu_custom_call" | custom-call | tf_op jit(solution)/shard_map/hand_out/pallas_call | solution.py:361

commit v4 on v3

--- a/solution.py
+++ b/solution.py
@@ -28,13 +28,14 @@
 
 
 def layer_kernel(
-    q_ref, k_ref, v_ref, w_ref, g_ref, lists_ref, counts_ref,
+    q_hbm, k_hbm, v_hbm, w_hbm, g_hbm, lists_ref, counts_ref,
     out_ref, dq_ref, dk_ref, dv_ref, dw_ref,
+    q_ref, w_ref,
     kw, vw, bias, st, pt, dst, attn, ga, gfull,
     rs_send, rs_recv, rs_keep, rs2_send, rs2_recv,
     ret_send, ret_recv, own_grad, relay, relay2,
     part32, part, ax, as1, az, ay, agz, agx, bz, bs1, bx, by, bgx, bgz,
-    halo_sem, head_sem, rs_sem, ret_sem, hop_sem, hop2_sem,
+    load_sem, halo_sem, head_sem, rs_sem, ret_sem, hop_sem, hop2_sem,
     sax, saz, say, taz, tax, sbz, sbx, sby, tbx, tbz,
 ):
     pos = lax.axis_index("ctx")
@@ -84,6 +85,8 @@
         started.append(c)
         return c
 
+    k_ref, v_ref = kw.at[ROWS : 2 * ROWS], vw.at[ROWS : 2 * ROWS]
+    g_ref = gfull.at[:, span(hi, 256)]
     barrier = pltpu.get_barrier_semaphore()
     peers = [right, left, to_mate, up, down]
     peers += [x_peer(d)[1] for d in range(1, NX)]
@@ -91,10 +94,14 @@
     peers += [y_peer(d)[1] for d in range(1, NY)]
     for device in peers:
         pl.semaphore_signal(barrier, inc=1, device_id=device, device_id_type=MESH)
-
-    kw[ROWS : 2 * ROWS] = k_ref[...]
-    vw[ROWS : 2 * ROWS] = v_ref[...]
-    gfull[:, span(hi, 256)] = g_ref[...]
+    pairs = ((k_hbm, k_ref), (v_hbm, v_ref), (g_hbm, g_ref), (q_hbm, q_ref), (w_hbm, w_ref))
+    loads = [
+        pltpu.make_async_copy(a, b, load_sem.at[i]) for i, (a, b) in enumerate(pairs)
+    ]
+    for c in loads:
+        c.start()
+    for c in loads:
+        c.wait()
     pl.semaphore_wait(barrier, len(peers))
 
     halo = [
@@ -252,7 +259,7 @@
             dk, dv = key_grads(h, side)
             ret_send[i, 0, :, hc] = dk.astype(BF)
             ret_send[i, 1, :, hc] = dv.astype(BF)
-        rets.append(send(ret_send.at[i], ret_recv.at[i], ret_sem, i, device))
+        rets.append(send(ret_send.at[i, 0], ret_recv.at[i, 0], ret_sem, i, device))
 
     def total_of(first, copies, slots):
         value = first.astype(F32)
@@ -271,6 +278,8 @@
     for d in range(1, NX):
         p, device = x_peer(d)
         b_x.append(send(bs1.at[:, span(p, 128)], bx.at[d - 1], sbx, d - 1, device))
+    for i, device in ((0, right), (1, left)):
+        rets.append(send(ret_send.at[i, 1], ret_recv.at[i, 1], ret_sem, 2 + i, device))
     pass_on2(0)
     pass_on2(2)
 
@@ -305,16 +314,32 @@
     agz[span(z, 32)] = y_total(a_y, ay)
     view = agz.at[span(z, 32)]
     a_gz = [send(view, view, taz, d - 1, z_peer(d)[1]) for d in range(1, NZ)]
+    a_gx, b_gz = [], []
+
+    def a_on(e):
+        rows = span((z + NZ - e) % NZ, 32)
+        for d in range(1, NX):
+            to = agx.at[rows, span(x, 128)]
+            a_gx.append(send(agz.at[rows], to, tax, e * (NX - 1) + d - 1, x_peer(d)[1]))
+
+    def b_on(e):
+        cols = span((x + NX - e) % NX, 128)
+        for d in (4, 3, 5, 2, 6, 1, 7):
+            to = bgz.at[span(z, 32), cols]
+            b_gz.append(send(bgx.at[:, cols], to, tbz, e * (NZ - 1) + d - 1, z_peer(d)[1]))
+
     bgx[:, span(x, 128)] = y_total(b_y, by)
     view_b = bgx.at[:, span(x, 128)]
     b_gx = [send(view_b, view_b, tbx, d - 1, x_peer(d)[1]) for d in range(1, NX)]
-    for c in b_gx:
-        c.wait_recv()
-    b_gz = [send(bgx, bgz.at[span(z, 32)], tbz, d - 1, z_peer(d)[1]) for d in range(1, NZ)]
+    b_on(0)
+    a_on(0)
+    for e in (1, 3, 2):
+        b_gx[e - 1].wait_recv()
+        b_on(e)
     bgz[span(z, 32)] = bgx[...]
-    for c in a_gz:
-        c.wait_recv()
-    a_gx = [send(agz, agx.at[:, span(x, 128)], tax, d - 1, x_peer(d)[1]) for d in range(1, NX)]
+    for e in (1, 7, 2, 6, 3, 5, 4):
+        a_gz[e - 1].wait_recv()
+        a_on(e)
     agx[:, span(x, 128)] = agz[...]
 
     for c in rs2:
@@ -377,9 +402,11 @@
     results = pl.pallas_call(
         layer_kernel,
         out_shape=(tok, tok, tok, tok, jax.ShapeDtypeStruct(out_weight.shape, F32)),
-        in_specs=[vmem] * 6 + [smem],
+        in_specs=[pl.BlockSpec(memory_space=pl.ANY)] * 5 + [vmem, smem],
         out_specs=[vmem] * 5,
         scratch_shapes=[
+            pltpu.VMEM((ROWS, 256), BF),
+            pltpu.VMEM((256, 1024), BF),
             pltpu.VMEM((WINDOW, 256), BF),
             pltpu.VMEM((WINDOW, 256), BF),
             pltpu.VMEM((16, ROWS), F32),
@@ -413,9 +440,9 @@
             pltpu.VMEM((NY, 32, 128), BF),
             pltpu.VMEM((32, 512), BF),
             pltpu.VMEM((256, 512), BF),
-            dma(4), dma(6), dma(2), dma(2), dma(8), dma(8),
-            dma(NX - 1), dma(NZ - 1), dma(NY - 1), dma(NZ - 1), dma(NX - 1),
-            dma(NZ - 1), dma(NX - 1), dma(NY - 1), dma(NX - 1), dma(NZ - 1),
+            pltpu.SemaphoreType.DMA((5,)), dma(4), dma(6), dma(2), dma(4), dma(8), dma(8),
+            dma(NX - 1), dma(NZ - 1), dma(NY - 1), dma(NZ - 1), dma(NZ * (NX - 1)),
+            dma(NZ - 1), dma(NX - 1), dma(NY - 1), dma(NX - 1), dma(NX * (NZ - 1)),
         ],
         compiler_params=pltpu.CompilerParams(
             collective_id=0, has_side_effects=True, vmem_limit_bytes=62 * 1024 * 1024

time: 86.5 us -> 88.9 us (1.028)
  Pallas kernels: 84.8 us -> 88 us
    pallas_call x1, Pallas kernels: 82.2 us -> 85.4 us  [shards(): pl.pallas_call(layer_kernel, out_shape=(tok, tok, tok, tok, jax.ShapeDtyp...]
where the time goes in v4:
time: 88.9 us; the launch traced here: 88.6 us
  Pallas kernels  88 us (99%)
    pallas_call x1, Pallas kernels, shards(): pl.pallas_call(layer_kernel, out_shape=(tok, tok, tok, tok, jax.ShapeDtyp...  85.4 us
    pallas_call x1, Pallas kernels, hand_out(): pl.pallas_call(hand_out_kernel, out_shape=shapes, in_specs=[hbm] * n, out...  2.61 us

profile of v4, /device:TPU:1, one launch (start us, length us, event | category | flops | bytes accessed | tf_op | source)
XLA Modules:
  0.0 88.6 jit_solution(13346406704755791850)
XLA Ops:
  0.6 85.4 %layer.1 = (bf16[512,256]{1,0:T(8,128)(2,1)}, bf16[512,256]{1,0:T(8,128)(2,1)}, bf16[512,256]{1,0:T(8,128)(2,1)}, bf16[512,256]{1,0:T(8,128)(2,1)}, f32[256,1024]{1,0:T(8,128)}) custom-call(bf16[512,256]{1,0:T(8,128)(2,1)} %q_hbm.1, bf16[512,256]{1,0:T(8,128)(2,1)} %k_hbm.1, bf16[512,256]{1,0:T(8,128)(2,1)} %v_hbm.1, bf16[256,1024]{1,0:T(8,128)(2,1)} %w_hbm.1, ...), custom_call_target="tpu_custom_call" | custom-call | tf_op jit(solution)/shard_map/layer/pallas_call | solution.py:402
  86.0 2.6 %hand_out.1 = (bf16[512,256]{1,0:T(8,128)(2,1)}, bf16[512,256]{1,0:T(8,128)(2,1)}, bf16[512,256]{1,0:T(8,128)(2,1)}, bf16[512,256]{1,0:T(8,128)(2,1)}, f32[256,1024]{1,0:T(8,128)}) custom-call(bf16[512,256]{1,0:T(8,128)(2,1)} %get-tuple-element.10.refs_0_, bf16[512,256]{1,0:T(8,128)(2,1)} %get-tuple-element.11.refs_1_, ...), custom_call_target="tpu_custom_call" | custom-call | tf_op jit(solution)/shard_map/hand_out/pallas_call | solution.py:386

commit v5 on v4

--- a/solution.py
+++ b/solution.py
@@ -260,6 +260,7 @@
             ret_send[i, 0, :, hc] = dk.astype(BF)
             ret_send[i, 1, :, hc] = dv.astype(BF)
         rets.append(send(ret_send.at[i, 0], ret_recv.at[i, 0], ret_sem, i, device))
+        rets.append(send(ret_send.at[i, 1], ret_recv.at[i, 1], ret_sem, 2 + i, device))
 
     def total_of(first, copies, slots):
         value = first.astype(F32)
@@ -278,8 +279,6 @@
     for d in range(1, NX):
         p, device = x_peer(d)
         b_x.append(send(bs1.at[:, span(p, 128)], bx.at[d - 1], sbx, d - 1, device))
-    for i, device in ((0, right), (1, left)):
-        rets.append(send(ret_send.at[i, 1], ret_recv.at[i, 1], ret_sem, 2 + i, device))
     pass_on2(0)
     pass_on2(2)
 

time: 88.9 us -> 87.2 us (0.981)
  Pallas kernels: 88 us -> 85.6 us
    pallas_call x1, Pallas kernels: 85.4 us -> 83 us  [shards(): pl.pallas_call(layer_kernel, out_shape=(tok, tok, tok, tok, jax.ShapeDtyp...]
where the time goes in v5:
time: 87.2 us; the launch traced here: 86.2 us
  Pallas kernels  85.6 us (98%)
    pallas_call x1, Pallas kernels, shards(): pl.pallas_call(layer_kernel, out_shape=(tok, tok, tok, tok, jax.ShapeDtyp...  83 us
    pallas_call x1, Pallas kernels, hand_out(): pl.pallas_call(hand_out_kernel, out_shape=shapes, in_specs=[hbm] * n, out...  2.61 us

profile of v5, /device:TPU:1, one launch (start us, length us, event | category | flops | bytes accessed | tf_op | source)
XLA Modules:
  0.0 86.2 jit_solution(15023511005281450831)
XLA Ops:
  0.6 83.0 %layer.1 = (bf16[512,256]{1,0:T(8,128)(2,1)}, bf16[512,256]{1,0:T(8,128)(2,1)}, bf16[512,256]{1,0:T(8,128)(2,1)}, bf16[512,256]{1,0:T(8,128)(2,1)}, f32[256,1024]{1,0:T(8,128)}) custom-call(bf16[512,256]{1,0:T(8,128)(2,1)} %q_hbm.1, bf16[512,256]{1,0:T(8,128)(2,1)} %k_hbm.1, bf16[512,256]{1,0:T(8,128)(2,1)} %v_hbm.1, bf16[256,1024]{1,0:T(8,128)(2,1)} %w_hbm.1, ...), custom_call_target="tpu_custom_call" | custom-call | tf_op jit(solution)/shard_map/layer/pallas_call | solution.py:401
  83.6 2.6 %hand_out.1 = (bf16[512,256]{1,0:T(8,128)(2,1)}, bf16[512,256]{1,0:T(8,128)(2,1)}, bf16[512,256]{1,0:T(8,128)(2,1)}, bf16[512,256]{1,0:T(8,128)(2,1)}, f32[256,1024]{1,0:T(8,128)}) custom-call(bf16[512,256]{1,0:T(8,128)(2,1)} %get-tuple-element.10.refs_0_, bf16[512,256]{1,0:T(8,128)(2,1)} %get-tuple-element.11.refs_1_, ...), custom_call_target="tpu_custom_call" | custom-call | tf_op jit(solution)/shard_map/hand_out/pallas_call | solution.py:385

commit v6 on v5

--- a/solution.py
+++ b/solution.py
@@ -110,9 +110,6 @@
     ]
     quarter = lambda c: slice(c * BLK, (c + 1) * BLK)
     hops = [None] * 4
-    for c in (0, 2, 1, 3):
-        device = up if c < 2 else down
-        hops[c] = send(g_ref.at[quarter(c)], relay.at[c], hop_sem, c, device)
     halo += [
         send(v_ref, vw.at[0:ROWS], halo_sem, 2, right),
         send(v_ref, vw.at[2 * ROWS : 3 * ROWS], halo_sem, 3, left),
@@ -155,14 +152,13 @@
     for h in range(HEADS_HERE):
         for c in (2, 3):
             score_chunk(h, c)
-    pass_on(0)
-    pass_on(2)
     halo[0].wait_recv()
+    for c in (0, 2, 1, 3):
+        device = up if c < 2 else down
+        hops[c] = send(g_ref.at[quarter(c)], relay.at[c], hop_sem, c, device)
     for h in range(HEADS_HERE):
         for c in (0, 1):
             score_chunk(h, c)
-    pass_on(1)
-    pass_on(3)
     halo[1].wait_recv()
     for h in range(HEADS_HERE):
         for c in (4, 5):
@@ -179,8 +175,12 @@
         for c in range(WINDOW // CHUNK):
             keys = slice(c * CHUNK, (c + 1) * CHUNK)
             pt[h, keys] = (st[h, keys] * inverse).astype(BF)
+    pass_on(0)
+    pass_on(2)
     halo[2].wait_recv()
     halo[3].wait_recv()
+    pass_on(1)
+    pass_on(3)
     attn_t = []
     for h in range(HEADS_HERE):
         hc = slice(h * HD, (h + 1) * HD)
@@ -313,32 +313,16 @@
     agz[span(z, 32)] = y_total(a_y, ay)
     view = agz.at[span(z, 32)]
     a_gz = [send(view, view, taz, d - 1, z_peer(d)[1]) for d in range(1, NZ)]
-    a_gx, b_gz = [], []
-
-    def a_on(e):
-        rows = span((z + NZ - e) % NZ, 32)
-        for d in range(1, NX):
-            to = agx.at[rows, span(x, 128)]
-            a_gx.append(send(agz.at[rows], to, tax, e * (NX - 1) + d - 1, x_peer(d)[1]))
-
-    def b_on(e):
-        cols = span((x + NX - e) % NX, 128)
-        for d in (4, 3, 5, 2, 6, 1, 7):
-            to = bgz.at[span(z, 32), cols]
-            b_gz.append(send(bgx.at[:, cols], to, tbz, e * (NZ - 1) + d - 1, z_peer(d)[1]))
-
     bgx[:, span(x, 128)] = y_total(b_y, by)
     view_b = bgx.at[:, span(x, 128)]
     b_gx = [send(view_b, view_b, tbx, d - 1, x_peer(d)[1]) for d in range(1, NX)]
-    b_on(0)
-    a_on(0)
-    for e in (1, 3, 2):
-        b_gx[e - 1].wait_recv()
-        b_on(e)
+    for c in b_gx:
+        c.wait_recv()
+    b_gz = [send(bgx, bgz.at[span(z, 32)], tbz, d - 1, z_peer(d)[1]) for d in range(1, NZ)]
     bgz[span(z, 32)] = bgx[...]
-    for e in (1, 7, 2, 6, 3, 5, 4):
-        a_gz[e - 1].wait_recv()
-        a_on(e)
+    for c in a_gz:
+        c.wait_recv()
+    a_gx = [send(agz, agx.at[:, span(x, 128)], tax, d - 1, x_peer(d)[1]) for d in range(1, NX)]
     agx[:, span(x, 128)] = agz[...]
 
     for c in rs2:

time: 87.2 us -> 85.5 us (0.981)
  Pallas kernels: 85.6 us -> 83.5 us
    pallas_call x1, Pallas kernels: 83 us -> 80.9 us  [shards(): pl.pallas_call(layer_kernel, out_shape=(tok, tok, tok, tok, jax.ShapeDtyp...]
where the time goes in v6:
time: 85.5 us; the launch traced here: 84.1 us
  Pallas kernels  83.5 us (98%)
    pallas_call x1, Pallas kernels, shards(): pl.pallas_call(layer_kernel, out_shape=(tok, tok, tok, tok, jax.ShapeDtyp...  80.9 us
    pallas_call x1, Pallas kernels, hand_out(): pl.pallas_call(hand_out_kernel, out_shape=shapes, in_specs=[hbm] * n, out...  2.61 us

profile of v6, /device:TPU:1, one launch (start us, length us, event | category | flops | bytes accessed | tf_op | source)
XLA Modules:
  0.0 84.1 jit_solution(14856668618130509419)
XLA Ops:
  0.6 80.9 %layer.1 = (bf16[512,256]{1,0:T(8,128)(2,1)}, bf16[512,256]{1,0:T(8,128)(2,1)}, bf16[512,256]{1,0:T(8,128)(2,1)}, bf16[512,256]{1,0:T(8,128)(2,1)}, f32[256,1024]{1,0:T(8,128)}) custom-call(bf16[512,256]{1,0:T(8,128)(2,1)} %q_hbm.1, bf16[512,256]{1,0:T(8,128)(2,1)} %k_hbm.1, bf16[512,256]{1,0:T(8,128)(2,1)} %v_hbm.1, bf16[256,1024]{1,0:T(8,128)(2,1)} %w_hbm.1, ...), custom_call_target="tpu_custom_call" | custom-call | tf_op jit(solution)/shard_map/layer/pallas_call | solution.py:385
  81.5 2.6 %hand_out.1 = (bf16[512,256]{1,0:T(8,128)(2,1)}, bf16[512,256]{1,0:T(8,128)(2,1)}, bf16[512,256]{1,0:T(8,128)(2,1)}, bf16[512,256]{1,0:T(8,128)(2,1)}, f32[256,1024]{1,0:T(8,128)}) custom-call(bf16[512,256]{1,0:T(8,128)(2,1)} %get-tuple-element.10.refs_0_, bf16[512,256]{1,0:T(8,128)(2,1)} %get-tuple-element.11.refs_1_, ...), custom_call_target="tpu_custom_call" | custom-call | tf_op jit(solution)/shard_map/hand_out/pallas_call | solution.py:369
